TPU v7x, 32 devices: a whole 2x2x4 slice. The times are simulated.
32 devices in a mesh: dp: 4 (over y, core), mp: 8 (over z, x).
Axes of the slice: x: 2, y: 2, z: 4, core: 2. Of those that a mesh axis runs over, the one named last changes fastest.
Arguments:
- pair_tokens: bfloat16 [64, 48, 8192], P('dp', None, 'mp'), may hold values from -6 to 6
- norm_gain: float32 [8192], replicated, may hold values from 0.1 to 1.9
- q_weight: bfloat16 [8192, 4096], P('dp', 'mp'), may hold values from -1.5 to 1.5
- k_weight: bfloat16 [8192, 1024], P('dp', 'mp'), may hold values from -1.5 to 1.5
- value_weight: bfloat16 [8192, 1024], P('dp', 'mp'), may hold values from -0.0625 to 0.0625
- o_weight: bfloat16 [4096, 8192], P('mp', 'dp'), may hold values from -0.375 to 0.375
- pair_row: int32 [64], replicated, may hold values from 0 to 15, as said below
- pair_span: int32 [64, 2], replicated, may hold values from 0 to 128, as said below
- block_ids: int32 [2048], P('dp'), may hold values from 0 to 11, as said below
Outputs:
- attn_out: bfloat16 [2048, 8192], P('dp', 'mp')
Inputs may be any that keep to these rules, and one draw needn't show every extreme that they name: `pair_row`: every packed row is tiled exactly by the spans of the pairs that name it; the pairs listed on one index of dp that name rows of one index of dp number at most 4, and 4 is reached. `pair_span`: each span holds one pair, start before end; end - start is at least 3 and at most 48; 48 is reached in every row, and the last pair of every row ends at 128. `block_ids`: the pair's place counts the pairs of its row in order of position; roles are 0 prompt, 1 chosen, 2 rejected, in that order within each pair, each present; consistent with pair_row and pair_span.
All inputs are finite; a program needn't handle non-finite values.
Results may differ from a plain program's by a relative error of at most 0.013.
Values may be sent and summed in bfloat16 or wider, within the bound.
A program may use at most 128 MiB of HBM per device.

v0:
```python
import functools

import jax
import jax.numpy as jnp
import numpy as np
from jax import lax
from jax.experimental import pallas as pl
from jax.experimental.pallas import tpu as pltpu
from jax.sharding import PartitionSpec as P

HEAD_SIZE = 128
ROW_TOKENS = 128
QUERY_PER_KV = 4
PIECES = 2
SLICES = 4
MESH = pl.DeviceIdType.MESH


def ring_member(place, count):
    place = lax.rem(place + 2 * count, count)
    return jnp.where(place < count // 2, 2 * place, 2 * (count - 1 - place) + 1)


def pieces_of_output(n_mp, width, chunk):
    if width != 2 * chunk:
        return 1
    order = list(range(0, n_mp, 2)) + list(range(1, n_mp, 2))[::-1]
    apart = all(order[p - 1] // 2 != order[(p + 1) % n_mp] // 2 for p in range(n_mp))
    return 2 if apart else 1


def kernel(
    n_dp, n_mp,
    map_ref, tok_ref, gain_ref, q_ref, k_ref, v_ref, o_ref, ids_ref, freq_ref,
    out_ref,
    xin, xg, wq, wk, wv, wo, acc, square, attn, sums, terms, cos_ref, sin_ref, vis_ref, put_ref,
    own_sem, t_send, t_recv, w_send, w_recv, x_send, x_recv, s_send, s_recv,
):
    me_dp = lax.axis_index("dp")
    me_mp = lax.axis_index("mp")

    def place_of(g):
        return jnp.where(lax.rem(g, 2) == 0, g // 2, n_mp - 1 - g // 2)

    place = place_of(me_mp)
    sides = (ring_member(place + 1, n_mp), ring_member(place - 1, n_mp))
    groups = n_dp // 2
    core = lax.rem(me_dp, 2)
    partner = me_dp + 1 - 2 * core
    others = [lax.rem(me_dp + 2 * j, n_dp) for j in range(1, groups)]
    tokens, chunk = out_ref.shape
    half = tokens // 2
    piece = half // PIECES
    block = tok_ref.shape[0] // n_dp
    width = o_ref.shape[1]
    n_out = pieces_of_output(n_mp, width, chunk)

    barrier = pltpu.get_barrier_semaphore()
    for side in sides:
        pl.semaphore_signal(barrier, inc=1, device_id={"mp": side}, device_id_type=MESH)
    for j in range(1, n_dp):
        peer = lax.rem(me_dp + j, n_dp)
        pl.semaphore_signal(barrier, inc=1, device_id={"dp": peer}, device_id_type=MESH)
    pl.semaphore_wait(barrier, 2 + n_dp - 1)

    def token_rows(owner):
        return pl.ds(pl.multiple_of(owner * block, 16), block)

    slice_width = chunk // SLICES

    def token_slice(sub):
        return pl.ds(sub * slice_width, slice_width)

    def token_copy(j, sub):
        peer = lax.rem(me_dp + j, n_dp)
        return pltpu.make_async_remote_copy(
            src_ref=tok_ref.at[token_rows(peer), token_slice(sub)],
            dst_ref=xin.at[token_rows(me_dp), token_slice(sub)],
            send_sem=t_send.at[sub, j - 1],
            recv_sem=t_recv.at[sub, me_dp],
            device_id={"dp": peer},
            device_id_type=MESH,
        )

    def token_arrival(j, sub):
        peer = lax.rem(me_dp + j, n_dp)
        return pltpu.make_async_remote_copy(
            src_ref=tok_ref.at[token_rows(peer), token_slice(sub)],
            dst_ref=xin.at[token_rows(peer), token_slice(sub)],
            send_sem=t_send.at[sub, j - 1],
            recv_sem=t_recv.at[sub, peer],
            device_id={"dp": peer},
            device_id_type=MESH,
        )

    own_tokens = pltpu.make_async_copy(
        tok_ref.at[token_rows(me_dp), :], xin.at[token_rows(me_dp), :], own_sem.at[4]
    )
    for sub in range(SLICES):
        for j in range(1, n_dp):
            token_copy(j, sub).start()
    own_tokens.start()

    def hop_of(g):
        gap = lax.rem(place_of(g) - place + n_mp, n_mp)
        gap = jnp.where(gap == 0, n_mp, gap)
        return jnp.minimum(gap, jnp.where(gap == n_mp, n_mp, n_mp - gap))

    def out_columns(which, owner):
        if n_out == 1:
            return owner * 0
        later = (hop_of(2 * owner + 1) < hop_of(2 * owner)).astype(jnp.int32)
        return chunk * (later if which == 3 else 1 - later)

    def part(which, owner):
        if which >= 3:
            start = owner * width + out_columns(which, owner)
            return wo.at[:, pl.ds(pl.multiple_of(start, 128), width // n_out)]
        full = (wq, wk, wv)[which]
        depth = q_ref.shape[0]
        return full.at[pl.ds(pl.multiple_of(owner * depth, 16), depth), :]

    def shard(which):
        if which >= 3:
            start = out_columns(which, me_dp)
            return o_ref.at[:, pl.ds(pl.multiple_of(start, 128), width // n_out)]
        return (q_ref, k_ref, v_ref)[which]

    kinds = 3 + n_out

    def weight_copy(which, owner, source, slot, peer):
        return pltpu.make_async_remote_copy(
            src_ref=source,
            dst_ref=part(which, owner),
            send_sem=w_send.at[which, slot],
            recv_sem=w_recv.at[which, owner],
            device_id={"dp": peer},
            device_id_type=MESH,
        )

    def x_copy(step, way, sub):
        sign = -1 if way == 0 else 1
        chunk_of = ring_member(place + sign * step, n_mp)
        ref = xg.at[chunk_of, pl.ds(way * half, half), token_slice(sub)]
        return pltpu.make_async_remote_copy(
            src_ref=ref,
            dst_ref=ref,
            send_sem=x_send.at[way, sub, step],
            recv_sem=x_recv.at[way, sub, step],
            device_id={"mp": sides[way]},
            device_id_type=MESH,
        )

    def x_arrival(step, way, sub):
        sign = -1 if way == 0 else 1
        chunk_of = ring_member(place + sign * (step + 1), n_mp)
        ref = xg.at[chunk_of, pl.ds(way * half, half), token_slice(sub)]
        return pltpu.make_async_remote_copy(
            src_ref=ref,
            dst_ref=ref,
            send_sem=x_send.at[way, sub, step],
            recv_sem=x_recv.at[way, sub, step],
            device_id={"mp": sides[way]},
            device_id_type=MESH,
        )

    owns = [
        pltpu.make_async_copy(
            (q_ref, k_ref, v_ref)[w],
            part(w, me_dp),
            own_sem.at[w],
        )
        for w in range(3)
    ]
    owns.append(
        pltpu.make_async_copy(
            o_ref,
            wo.at[:, pl.ds(pl.multiple_of(me_dp * width, 128), width)],
            own_sem.at[3],
        )
    )
    def second_chunk(owner):
        return (owner * width + out_columns(4, owner)) // chunk

    def second_stage(owner):
        hop = hop_of(second_chunk(owner))
        return jnp.where(hop == n_mp, 2, jnp.where(hop > 2, 1, 0))

    held = second_stage(me_dp) == 2

    def send_second():
        for j, peer in enumerate(others):
            weight_copy(4, me_dp, shard(4), 1 + j, peer).start()

    for w in range(min(kinds, 4)):
        for j, peer in enumerate(others):
            weight_copy(w, me_dp, shard(w), 1 + j, peer).start()
    if kinds == 5:
        pl.when(jnp.logical_not(held))(send_second)
    for w in range(3):
        owns[w].start()
        weight_copy(w, me_dp, shard(w), 0, partner).start()

    def tables(r, carry):
        rows = pl.ds(pl.multiple_of(r * ROW_TOKENS, ROW_TOKENS), ROW_TOKENS)
        ids_j = jnp.broadcast_to(ids_ref[pl.ds(r, 1), :], (ROW_TOKENS, ROW_TOKENS)).astype(
            jnp.float32
        )
        ids_i = jnp.transpose(ids_j)
        pair_i = jnp.floor((ids_i + 0.5) * (1.0 / 3.0))
        pair_j = jnp.floor((ids_j + 0.5) * (1.0 / 3.0))
        at_i = lax.broadcasted_iota(jnp.int32, (ROW_TOKENS, ROW_TOKENS), 0)
        at_j = lax.broadcasted_iota(jnp.int32, (ROW_TOKENS, ROW_TOKENS), 1)
        hidden = (ids_i - 3.0 * pair_i == 2.0) & (ids_j - 3.0 * pair_j == 1.0)
        seen = jnp.where((at_j <= at_i) & (pair_i == pair_j), 1.0, 0.0)
        seen = jnp.where(hidden, 0.0, seen)
        vis_ref[rows, :] = seen
        angle = (jnp.sum(seen, axis=1, keepdims=True) - 1.0) * freq_ref[...]
        lane = lax.broadcasted_iota(jnp.int32, (ROW_TOKENS, HEAD_SIZE), 1)
        sine = jnp.sin(angle)
        cos_ref[rows, :] = jnp.cos(angle)
        sin_ref[rows, :] = jnp.where(lane < HEAD_SIZE // 2, -sine, sine)
        return carry

    lax.fori_loop(0, tokens // ROW_TOKENS, tables, 0)
    acc[...] = jnp.zeros_like(acc)
    square[...] = jnp.zeros_like(square)

    own_tokens.wait()
    at = lax.broadcasted_iota(jnp.int32, (tokens, n_dp * block), 0)
    put_ref[...] = jnp.where(at == map_ref[...], 1.0, 0.0).astype(jnp.bfloat16)
    for sub in range(SLICES):
        for j in range(1, n_dp):
            token_arrival(j, sub).wait_recv()
        columns = slice(sub * slice_width, (sub + 1) * slice_width)
        xg[me_mp, :, columns] = jnp.dot(
            put_ref[...], xin[:, columns], preferred_element_type=jnp.float32
        ).astype(jnp.bfloat16)
        for way in range(2):
            x_copy(0, way, sub).start()
    owns[3].start()
    for w in range(3, kinds):
        weight_copy(w, me_dp, shard(w), 0, partner).start()

    def pass_weight(w):
        for j in range(1, groups):
            owner = lax.rem(me_dp + n_dp - 2 * j, n_dp)
            weight_copy(w, owner, part(w, owner), 0, partner).wait_recv()
            weight_copy(w, owner, part(w, owner), groups + j - 1, partner).start()

    def weight_done(w):
        for i in range(groups):
            owner = lax.rem(partner + 2 * i, n_dp)
            weight_copy(w, owner, part(w, owner), 0, partner).wait_recv()

    q_width = wq.shape[1]
    k_width = wk.shape[1]

    def project(way, g):
        halves = pl.ds(pl.multiple_of(way * half, 16), half)
        wide = xg[g, halves, :].astype(jnp.float32)
        square[halves, :] += jnp.sum(wide * wide, axis=1, keepdims=True)
        columns = pl.ds(pl.multiple_of(g * chunk, 128), chunk)
        scaled = (wide * gain_ref[:, columns]).astype(jnp.bfloat16)
        rows = pl.ds(pl.multiple_of(g * chunk, 16), chunk)
        acc[halves, 0:q_width] += jnp.dot(
            scaled, wq[rows, :], preferred_element_type=jnp.float32
        )
        acc[halves, q_width:q_width + k_width] += jnp.dot(
            scaled, wk[rows, :], preferred_element_type=jnp.float32
        )
        acc[halves, q_width + k_width:] += jnp.dot(
            scaled, wv[rows, :], preferred_element_type=jnp.float32
        )

    def project_step(hop, near):
        def one(way, carry):
            g = ring_member(place + jnp.where(way == 0, -hop, hop), n_mp)
            is_near = (g * chunk) // (2 * q_ref.shape[0]) == me_dp // 2

            @pl.when(is_near == near)
            def _():
                project(way, g)

            return carry

        lax.fori_loop(0, 2, one, 0)

    for w in range(3):
        owns[w].wait()
        owner = partner
        weight_copy(w, owner, part(w, owner), 0, partner).wait_recv()

    def gather_step(step, carry):
        project_step(step, True)
        for sub in range(SLICES):
            for way in range(2):
                x_arrival(step, way, sub).wait_recv()
                x_copy(step + 1, way, sub).start()
        return carry

    def weight_rest(w):
        for i in range(1, groups):
            owner = lax.rem(partner + 2 * i, n_dp)
            weight_copy(w, owner, part(w, owner), 0, partner).wait_recv()

    late = max(n_mp - 3, 0)
    lax.fori_loop(0, late, gather_step, 0)
    pass_weight(0)
    lax.fori_loop(late, n_mp - 2, gather_step, 0)
    pass_weight(1)
    pass_weight(2)
    project_step(n_mp - 2, True)
    for w in range(3):
        weight_rest(w)

    def project_far(hop, carry):
        project_step(hop, False)
        return carry

    lax.fori_loop(0, n_mp - 1, project_far, 0)
    for sub in range(SLICES):
        for way in range(2):
            x_arrival(n_mp - 2, way, sub).wait_recv()

    def project_last(way, carry):
        project(way, ring_member(place + jnp.where(way == 0, 1 - n_mp, n_mp - 1), n_mp))
        return carry

    lax.fori_loop(0, 2, project_last, 0)
    acc[...] = acc[...] * lax.rsqrt(square[...] / (n_mp * chunk) + 1e-05)

    def turn(u, cosine, sine):
        return (u * cosine + pltpu.roll(u, HEAD_SIZE // 2, 1) * sine).astype(jnp.bfloat16)

    def attend(r, carry):
        rows = pl.ds(pl.multiple_of(r * ROW_TOKENS, ROW_TOKENS), ROW_TOKENS)
        cosine = cos_ref[rows, :]
        sine = sin_ref[rows, :]
        seen = vis_ref[rows, :] > 0.5
        for kv in range(k_width // HEAD_SIZE):
            at_k = q_width + kv * HEAD_SIZE
            key = turn(acc[rows, at_k:at_k + HEAD_SIZE], cosine, sine)
            value = acc[rows, at_k + k_width:at_k + k_width + HEAD_SIZE].astype(jnp.bfloat16)
            for h in range(kv * QUERY_PER_KV, (kv + 1) * QUERY_PER_KV):
                at = slice(h * HEAD_SIZE, (h + 1) * HEAD_SIZE)
                query = turn(acc[rows, at], cosine, sine)
                scores = lax.dot_general(
                    query, key, (((1,), (1,)), ((), ())), preferred_element_type=jnp.float32
                ) * HEAD_SIZE ** (-0.5)
                scores = jnp.where(seen, scores, -1e30)
                expo = jnp.exp(scores - jnp.max(scores, axis=-1, keepdims=True))
                probs = (expo / jnp.sum(expo, axis=-1, keepdims=True)).astype(jnp.bfloat16)
                attn[rows, at] = jnp.dot(
                    probs, value, preferred_element_type=jnp.float32
                ).astype(jnp.bfloat16)
        return carry

    lax.fori_loop(0, tokens // ROW_TOKENS, attend, 0)
    if kinds == 5:
        pl.when(held)(send_second)
    owns[3].wait()
    pass_weight(3)
    weight_done(3)

    def make_terms(hop):
        for way in range(2):
            sign = -1 if way == 0 else 1
            g = ring_member(place + sign * hop, n_mp)
            columns = pl.ds(pl.multiple_of(g * chunk, 128), chunk)
            terms[way] = jnp.dot(
                attn[way * half:(way + 1) * half, :],
                wo[:, columns],
                preferred_element_type=jnp.float32,
            )

    def sum_copy(slot, way, sub):
        rows = pl.ds(sub * piece, piece)
        return pltpu.make_async_remote_copy(
            src_ref=sums.at[way, slot, rows, :],
            dst_ref=sums.at[way, slot + 1, rows, :],
            send_sem=s_send.at[way, sub, slot],
            recv_sem=s_recv.at[way, sub, slot],
            device_id={"mp": sides[way]},
            device_id_type=MESH,
        )

    make_terms(1)
    for sub in range(PIECES):
        for way in range(2):
            rows = slice(sub * piece, (sub + 1) * piece)
            sums[way, 0, rows, :] = terms[way, rows, :].astype(jnp.bfloat16)
            sum_copy(0, way, sub).start()

    def second_pieces(stage):
        if kinds < 5:
            return
        for j in range(1, groups):
            owner = lax.rem(me_dp + n_dp - 2 * j, n_dp)

            @pl.when(second_stage(owner) == stage)
            def _():
                weight_copy(4, owner, part(4, owner), 0, partner).wait_recv()
                weight_copy(4, owner, part(4, owner), groups + j - 1, partner).start()

        for i in range(groups):
            owner = lax.rem(partner + 2 * i, n_dp)

            @pl.when(second_stage(owner) == stage)
            def _():
                weight_copy(4, owner, part(4, owner), 0, partner).wait_recv()

    second_pieces(0)

    def scatter_step(step, carry):
        @pl.when(step == 1)
        def _():
            second_pieces(1)

        make_terms(step + 2)
        for sub in range(PIECES):
            for way in range(2):
                sum_copy(step, way, sub).wait_recv()
                rows = slice(sub * piece, (sub + 1) * piece)
                total = sums[way, step + 1, rows, :].astype(jnp.float32) + terms[way, rows, :]
                sums[way, step + 1, rows, :] = total.astype(jnp.bfloat16)
                sum_copy(step + 1, way, sub).start()
        return carry

    lax.fori_loop(0, n_mp - 2, scatter_step, 0)
    second_pieces(2)
    make_terms(n_mp)
    for sub in range(PIECES):
        for way in range(2):
            sum_copy(n_mp - 2, way, sub).wait_recv()
            rows = slice(sub * piece, (sub + 1) * piece)
            total = sums[way, n_mp - 1, rows, :].astype(jnp.float32) + terms[way, rows, :]
            start = way * half + sub * piece
            out_ref[start:start + piece, :] = total.astype(jnp.bfloat16)

    def drain(step, carry):
        for way in range(2):
            for sub in range(SLICES):
                x_copy(step, way, sub).wait_send()
            for sub in range(PIECES):
                sum_copy(step, way, sub).wait_send()
        return carry

    lax.fori_loop(0, n_mp - 1, drain, 0)
    for sub in range(SLICES):
        for j in range(1, n_dp):
            token_copy(j, sub).wait_send()
    for w in range(kinds):
        for i in range(2 * groups - 1):
            weight_copy(w, me_dp, shard(w), i, partner).wait_send()


def local(
    pair_tokens,
    norm_gain,
    q_weight,
    k_weight,
    value_weight,
    o_weight,
    pair_row,
    pair_span,
    block_ids,
):
    dp_count = lax.axis_size("dp")
    mp_count = lax.axis_size("mp")
    own_index = lax.axis_index("dp")
    pairs_dev = pair_tokens.shape[0]
    pair_cap = pair_tokens.shape[1]
    width_local = pair_tokens.shape[2]
    all_pairs = pair_row.shape[0]
    most_sent = -(-pairs_dev // dp_count)
    tok_dev = block_ids.shape[0]
    rows_dev = tok_dev // ROW_TOKENS
    owners_all = (pair_row // rows_dev).reshape(dp_count, pairs_dev)
    same_owner = owners_all[:, :, None] == owners_all[:, None, :]
    listed = jnp.arange(pairs_dev)
    before = listed[None, :] < listed[:, None]
    rank_all = jnp.sum((same_owner & before[None]).astype(jnp.int32), axis=2)
    own_owner = lax.dynamic_index_in_dim(owners_all, own_index, 0, keepdims=False)
    own_rank = lax.dynamic_index_in_dim(rank_all, own_index, 0, keepdims=False)
    slots = jnp.arange(pair_cap, dtype=jnp.int32)
    sent = dp_count * most_sent
    own_slot = ((own_owner * most_sent + own_rank)[:, None] * pair_cap + slots[None, :]).reshape(-1)
    pick = (jnp.arange(sent * pair_cap)[:, None] == own_slot[None, :]).astype(jnp.bfloat16)
    outgoing = jnp.dot(
        pick,
        pair_tokens.reshape(pairs_dev * pair_cap, width_local),
        preferred_element_type=jnp.float32,
    ).astype(jnp.bfloat16)
    length = pair_span[:, 1] - pair_span[:, 0]
    source = jnp.arange(all_pairs, dtype=jnp.int32) // pairs_dev
    first = (pair_row % rows_dev) * ROW_TOKENS + pair_span[:, 0]
    place = source * most_sent + rank_all.reshape(-1)
    mine = owners_all.reshape(-1) == own_index
    match = (jnp.arange(sent)[:, None] == place[None, :]) & mine[None, :]
    first_of = jnp.sum(jnp.where(match, first[None, :], 0), axis=1)
    length_of = jnp.sum(jnp.where(match, length[None, :], 0), axis=1)
    placement_map = jnp.where(
        slots[None, :] < length_of[:, None], first_of[:, None] + slots[None, :], tok_dev
    ).reshape(-1)
    half = HEAD_SIZE // 2
    freq = 500000.0 ** (-(np.arange(half, dtype=np.float32) * 2.0 / HEAD_SIZE))
    freq = np.concatenate([freq, freq])[None, :].astype(np.float32)

    q_width = q_weight.shape[1]
    k_width = k_weight.shape[1]
    width = norm_gain.shape[0]
    far = dp_count - 1
    vmem = pl.BlockSpec(memory_space=pltpu.VMEM)
    anyspace = pl.BlockSpec(memory_space=pl.ANY)
    bf16 = jnp.bfloat16
    return pl.pallas_call(
        functools.partial(kernel, dp_count, mp_count),
        out_shape=jax.ShapeDtypeStruct((tok_dev, width_local), bf16),
        in_specs=[vmem, anyspace, vmem, anyspace, anyspace, anyspace, anyspace, vmem, vmem],
        out_specs=vmem,
        scratch_shapes=[
            pltpu.VMEM((sent * pair_cap, width_local), bf16),
            pltpu.VMEM((mp_count, tok_dev, width_local), bf16),
            pltpu.VMEM((width, q_width), bf16),
            pltpu.VMEM((width, k_width), bf16),
            pltpu.VMEM((width, k_width), bf16),
            pltpu.VMEM((o_weight.shape[0], width), bf16),
            pltpu.VMEM((tok_dev, q_width + 2 * k_width), jnp.float32),
            pltpu.VMEM((tok_dev, 1), jnp.float32),
            pltpu.VMEM((tok_dev, q_width), bf16),
            pltpu.VMEM((2, mp_count, tok_dev // 2, width_local), bf16),
            pltpu.VMEM((2, tok_dev // 2, width_local), jnp.float32),
            pltpu.VMEM((tok_dev, HEAD_SIZE), jnp.float32),
            pltpu.VMEM((tok_dev, HEAD_SIZE), jnp.float32),
            pltpu.VMEM((tok_dev, ROW_TOKENS), jnp.float32),
            pltpu.VMEM((tok_dev, sent * pair_cap), bf16),
            pltpu.SemaphoreType.DMA((5,)),
            pltpu.SemaphoreType.DMA((SLICES, far)),
            pltpu.SemaphoreType.DMA((SLICES, dp_count)),
            pltpu.SemaphoreType.DMA((5, far)),
            pltpu.SemaphoreType.DMA((5, dp_count)),
            pltpu.SemaphoreType.DMA((2, SLICES, mp_count - 1)),
            pltpu.SemaphoreType.DMA((2, SLICES, mp_count - 1)),
            pltpu.SemaphoreType.DMA((2, PIECES, mp_count - 1)),
            pltpu.SemaphoreType.DMA((2, PIECES, mp_count - 1)),
        ],
        compiler_params=pltpu.CompilerParams(
            collective_id=0, has_side_effects=True, vmem_limit_bytes=60 * 1024 * 1024
        ),
    )(
        placement_map[None, :],
        outgoing,
        norm_gain[None, :],
        q_weight,
        k_weight,
        value_weight,
        o_weight,
        block_ids.reshape(rows_dev, ROW_TOKENS),
        jnp.asarray(freq),
    )


def solution(mesh):
    placed = (
        P("dp", None, "mp"),
        P(),
        P("dp", "mp"),
        P("dp", "mp"),
        P("dp", "mp"),
        P("mp", "dp"),
        P(),
        P(),
        P("dp"),
    )
    return jax.shard_map(
        local, mesh=mesh, in_specs=placed, out_specs=P("dp", "mp"), check_vma=False
    )
```

profile of v0, /device:TPU:15, one launch (start us, length us, event | category | flops | bytes accessed | tf_op | source)
XLA Modules:
  0.0 214.9 jit_solution(17657539233362236046)
XLA Ops:
  0.0 0.0 copy-start
  0.0 1.4 copy-done
  1.4 0.7 broadcast_compare_fusion
  2.1 0.1 eq.50
  2.2 0.2 convert_reduce_fusion
  2.4 0.1 reshape.136
  2.5 0.8 fusion.7
  3.3 0.1 select_reduce_fusion.1
  3.4 0.1 add_select_fusion
  3.4 0.7 select_n.51.map_ref
  4.1 0.1 iota_add_fusion
  4.2 0.1 add.81
  4.3 2.5 %fusion.1.tok_ref = bf16[768,1024]{1,0:T(8,128)(2,1)} fusion(bf16[768,1024]{1,0:T(8,128)(2,1)S(1)} %bitcast.11, s32[768]{0:T(1024)S(1)} %add.81), kind=kOutput, calls=%fused_computation.2 | convolution fusion | flops 1209335808 | bytes 3148800 | tf_op jit(solution)/shard_map/dot_general | solution.py:490
  6.8 205.9 %shard_map.100 = bf16[512,1024]{1,0:T(8,128)(2,1)} custom-call(s32[1,768]{1,0:T(1,128)} %select_n.51.map_ref, bf16[768,1024]{1,0:T(8,128)(2,1)} %fusion.1.tok_ref, f32[1,8192]{1,0:T(1,128)} %bitcast.12, bf16[2048,512]{1,0:T(8,128)(2,1)} %q_ref.1, bf16[2048,128]{1,0:T(8,128)(2,1)} %k_ref.1, bf16[2048,128]{1,0:T(8,128)(2,1)} %v_ref.1, ...), custom_call_target="tpu_custom_call" | custom-call | tf_op jit(solution)/shard_map/pallas_call | solution.py:517
  212.7 2.3 %copy.12 = bf16[512,1024]{1,0:T(8,128)(2,1)} copy(bf16[512,1024]{1,0:T(8,128)(2,1)} %shard_map.100) | data formatting | bytes 2097152
  (2 shorter events, 0.0 us)
Async XLA Ops:
  0.0 1.4 copy-start
where the time goes:
time: 218 us; the launch traced here: 215 us
  Pallas kernels  206 us (94%)
  local copies, waits for them, and re-layouts  4.58 us (2%)
  matrix products  2.54 us (1%)
    pallas_call x1, Pallas kernels, local(): pl.pallas_call(functools.partial(kernel, dp_count, mp_count), out_shape=j...  206 us

commit v1 on v0

v1 whole, which is shorter than its diff:
```python
import functools

import jax
import jax.numpy as jnp
import numpy as np
from jax import lax
from jax.experimental import pallas as pl
from jax.experimental.pallas import tpu as pltpu
from jax.sharding import PartitionSpec as P

HEAD_SIZE = 128
ROW_TOKENS = 128
QUERY_PER_KV = 4
SLICES = 4
PARTS = 4
COLUMNS = 4
UNITS = 2
MESH = pl.DeviceIdType.MESH


def ring_member(place, count):
    place = lax.rem(place + 2 * count, count)
    return jnp.where(place < count // 2, 2 * place, 2 * (count - 1 - place) + 1)


def pieces_of_output(n_mp, width, chunk):
    if width != 2 * chunk:
        return 1
    order = list(range(0, n_mp, 2)) + list(range(1, n_mp, 2))[::-1]
    apart = all(order[p - 1] // 2 != order[(p + 1) % n_mp] // 2 for p in range(n_mp))
    return 2 if apart else 1


def kernel(
    n_dp, n_mp,
    row_ref, span_ref, tok_ref, gain_ref, q_ref, k_ref, v_ref, o_ref, ids_ref, freq_ref,
    out_ref,
    tokv, xout, xin, xg, wall, wo, acc, square, attn, sums, terms, cos_ref, sin_ref, vis_ref,
    put_ref, pick, first_of, length_of,
    own_sem, t_send, t_recv, w_send, w_recv, x_send, x_recv, s_send, s_recv,
):
    me_dp = lax.axis_index("dp")
    me_mp = lax.axis_index("mp")

    def place_of(g):
        return jnp.where(lax.rem(g, 2) == 0, g // 2, n_mp - 1 - g // 2)

    place = place_of(me_mp)
    sides = (ring_member(place + 1, n_mp), ring_member(place - 1, n_mp))
    groups = n_dp // 2
    core = lax.rem(me_dp, 2)
    group = me_dp // 2
    partner = me_dp + 1 - 2 * core
    others = [lax.rem(me_dp + 2 * j, n_dp) for j in range(1, groups)]
    tokens, chunk = out_ref.shape
    half = tokens // 2
    rows_dev = tokens // ROW_TOKENS
    pairs_dev, cap, _ = tok_ref.shape
    most = -(-pairs_dev // n_dp)
    slots = n_dp * most
    block = most * cap
    depth, q_width = q_ref.shape
    k_width = k_ref.shape[1]
    width = o_ref.shape[1]
    n_out = pieces_of_output(n_mp, width, chunk)
    slice_width = chunk // SLICES
    part_rows = depth // PARTS
    unit = chunk // UNITS
    column = chunk // COLUMNS
    out_column = width // n_out // COLUMNS
    base = 3 * PARTS
    kinds = base + n_out * COLUMNS
    last = n_mp - 1
    part_stage = [min(2, last), min(4, last), min(5, last), last]

    def token_slice(sub):
        return pl.ds(pl.multiple_of(sub * slice_width, 128), slice_width)

    own_tokens = pltpu.make_async_copy(tok_ref, tokv, own_sem.at[4])
    own_tokens.start()

    barrier = pltpu.get_barrier_semaphore()
    for side in sides:
        pl.semaphore_signal(barrier, inc=1, device_id={"mp": side}, device_id_type=MESH)
    for j in range(1, n_dp):
        peer = lax.rem(me_dp + j, n_dp)
        pl.semaphore_signal(barrier, inc=1, device_id={"dp": peer}, device_id_type=MESH)

    owner_list = [lax.div(row_ref[me_dp * pairs_dev + p], rows_dev) for p in range(pairs_dev)]
    slot_list = []
    for p in range(pairs_dev):
        rank = jnp.int32(0)
        for e in range(p):
            rank = rank + jnp.where(owner_list[e] == owner_list[p], 1, 0)
        slot_list.append(owner_list[p] * most + rank)
    for s in range(slots):
        index = jnp.int32(0)
        for p in range(1, pairs_dev):
            index = jnp.where(slot_list[p] == s, p, index)
        pick[s] = index

    pl.semaphore_wait(barrier, 2 + n_dp - 1)

    def token_rows(owner):
        return pl.ds(pl.multiple_of(owner * block, 16), block)

    def token_copy(j, sub, landing):
        peer = lax.rem(me_dp + j, n_dp)
        return pltpu.make_async_remote_copy(
            src_ref=xout.at[token_rows(peer), token_slice(sub)],
            dst_ref=xin.at[token_rows(landing), token_slice(sub)],
            send_sem=t_send.at[sub, j - 1],
            recv_sem=t_recv.at[sub, landing],
            device_id={"dp": peer},
            device_id_type=MESH,
        )

    def send_tokens(sub, carry):
        def arrange(s, c):
            rows = pl.ds(pl.multiple_of(s * cap, 16), cap)
            xout[rows, token_slice(sub)] = tokv[pick[s], :, token_slice(sub)]
            return c

        lax.fori_loop(0, slots, arrange, 0)
        for j in range(1, n_dp):
            token_copy(j, sub, me_dp).start()
        xin[token_rows(me_dp), token_slice(sub)] = xout[token_rows(me_dp), token_slice(sub)]
        return carry

    own_tokens.wait()
    lax.fori_loop(0, SLICES, send_tokens, 0)

    def hop_of(g):
        gap = lax.rem(place_of(g) - place + n_mp, n_mp)
        gap = jnp.where(gap == 0, n_mp, gap)
        return jnp.minimum(gap, jnp.where(gap == n_mp, n_mp, n_mp - gap))

    def out_columns(second, owner):
        if n_out == 1:
            return owner * 0
        later = (hop_of(2 * owner + 1) < hop_of(2 * owner)).astype(jnp.int32)
        return chunk * (1 - later if second else later)

    starts = (0, q_width, q_width + k_width)
    spans = (q_width, k_width, k_width)

    def part(kind, owner):
        if kind >= base:
            second, c = divmod(kind - base, COLUMNS)
            start = owner * width + out_columns(second, owner) + c * out_column
            return wo.at[:, pl.ds(pl.multiple_of(start, 128), out_column)]
        p, which = divmod(kind, 3)
        start = owner * depth + p * part_rows
        return wall.at[
            pl.ds(pl.multiple_of(start, 16), part_rows), pl.ds(starts[which], spans[which])
        ]

    def shard(kind):
        if kind >= base:
            second, c = divmod(kind - base, COLUMNS)
            start = out_columns(second, me_dp) + c * out_column
            return o_ref.at[:, pl.ds(pl.multiple_of(start, 128), out_column)]
        p, which = divmod(kind, 3)
        return (q_ref, k_ref, v_ref)[which].at[pl.ds(p * part_rows, part_rows), :]

    def weight_copy(kind, owner, source, target, slot, peer):
        return pltpu.make_async_remote_copy(
            src_ref=source,
            dst_ref=target,
            send_sem=w_send.at[kind, slot],
            recv_sem=w_recv.at[kind, owner],
            device_id={"dp": peer},
            device_id_type=MESH,
        )

    def held_copy(kind, owner, slot):
        return weight_copy(kind, owner, part(kind, owner), part(kind, owner), slot, partner)

    def send_away(kind):
        for j, peer in enumerate(others):
            weight_copy(kind, me_dp, shard(kind), part(kind, me_dp), 1 + j, peer).start()

    def send_partner(kind):
        weight_copy(kind, me_dp, shard(kind), part(kind, me_dp), 0, partner).start()

    owns = [
        pltpu.make_async_copy(
            (q_ref, k_ref, v_ref)[w],
            wall.at[
                pl.ds(pl.multiple_of(me_dp * depth, 16), depth), pl.ds(starts[w], spans[w])
            ],
            own_sem.at[w],
        )
        for w in range(3)
    ]
    owns.append(
        pltpu.make_async_copy(
            o_ref,
            wo.at[:, pl.ds(pl.multiple_of(me_dp * width, 128), width)],
            own_sem.at[3],
        )
    )

    for kind in range(base // 2):
        send_away(kind)
    for w in range(3):
        owns[w].start()
    for kind in range(base):
        send_partner(kind)

    def x_copy(step, way, sub):
        sign = -1 if way == 0 else 1
        chunk_of = ring_member(place + sign * step, n_mp)
        ref = xg.at[chunk_of, pl.ds(way * half, half), token_slice(sub)]
        return pltpu.make_async_remote_copy(
            src_ref=ref,
            dst_ref=ref,
            send_sem=x_send.at[way, sub, step],
            recv_sem=x_recv.at[way, sub, step],
            device_id={"mp": sides[way]},
            device_id_type=MESH,
        )

    def x_arrival(step, way, sub):
        sign = -1 if way == 0 else 1
        chunk_of = ring_member(place + sign * (step + 1), n_mp)
        ref = xg.at[chunk_of, pl.ds(way * half, half), token_slice(sub)]
        return pltpu.make_async_remote_copy(
            src_ref=ref,
            dst_ref=ref,
            send_sem=x_send.at[way, sub, step],
            recv_sem=x_recv.at[way, sub, step],
            device_id={"mp": sides[way]},
            device_id_type=MESH,
        )

    def find_places(j, carry):
        firsts = [jnp.int32(0)] * most
        lengths = [jnp.int32(0)] * most
        found = jnp.int32(0)
        for p in range(pairs_dev):
            i = j * pairs_dev + p
            row = row_ref[i]
            begin = span_ref[i, 0]
            end = span_ref[i, 1]
            first = lax.rem(row, rows_dev) * ROW_TOKENS + begin
            spot = jnp.where(lax.div(row, rows_dev) == me_dp, found, most)
            for k in range(most):
                firsts[k] = jnp.where(spot == k, first, firsts[k])
                lengths[k] = jnp.where(spot == k, end - begin, lengths[k])
            found = jnp.where(spot == most, found, found + 1)
        for k in range(most):
            first_of[j * most + k] = firsts[k]
            length_of[j * most + k] = lengths[k]
        return carry

    lax.fori_loop(0, n_dp, find_places, 0)
    lane = lax.broadcasted_iota(jnp.int32, (1, slots * cap), 1)
    target = jnp.full((1, slots * cap), tokens, jnp.int32)
    for s in range(slots):
        offset = lane - s * cap
        inside = (offset >= 0) & (offset < length_of[s])
        target = jnp.where(inside, offset + first_of[s], target)
    at = lax.broadcasted_iota(jnp.int32, (tokens, slots * cap), 0)
    put_ref[...] = jnp.where(at == target, 1.0, 0.0).astype(jnp.bfloat16)

    def tables(r, carry):
        rows = pl.ds(pl.multiple_of(r * ROW_TOKENS, ROW_TOKENS), ROW_TOKENS)
        ids_j = jnp.broadcast_to(ids_ref[pl.ds(r, 1), :], (ROW_TOKENS, ROW_TOKENS)).astype(
            jnp.float32
        )
        ids_i = jnp.transpose(ids_j)
        pair_i = jnp.floor((ids_i + 0.5) * (1.0 / 3.0))
        pair_j = jnp.floor((ids_j + 0.5) * (1.0 / 3.0))
        at_i = lax.broadcasted_iota(jnp.int32, (ROW_TOKENS, ROW_TOKENS), 0)
        at_j = lax.broadcasted_iota(jnp.int32, (ROW_TOKENS, ROW_TOKENS), 1)
        hidden = (ids_i - 3.0 * pair_i == 2.0) & (ids_j - 3.0 * pair_j == 1.0)
        seen = jnp.where((at_j <= at_i) & (pair_i == pair_j), 1.0, 0.0)
        seen = jnp.where(hidden, 0.0, seen)
        vis_ref[rows, :] = seen
        angle = (jnp.sum(seen, axis=1, keepdims=True) - 1.0) * freq_ref[...]
        lane_at = lax.broadcasted_iota(jnp.int32, (ROW_TOKENS, HEAD_SIZE), 1)
        sine = jnp.sin(angle)
        cos_ref[rows, :] = jnp.cos(angle)
        sin_ref[rows, :] = jnp.where(lane_at < HEAD_SIZE // 2, -sine, sine)
        return carry

    acc[...] = jnp.zeros_like(acc)
    square[...] = jnp.zeros_like(square)

    def ramp(sub, carry):
        for j in range(1, n_dp):
            token_copy(j, sub, lax.rem(me_dp + j, n_dp)).wait_recv()
        xg[me_mp, :, token_slice(sub)] = jnp.dot(
            put_ref[...], xin[:, token_slice(sub)], preferred_element_type=jnp.float32
        ).astype(jnp.bfloat16)
        for way in range(2):
            x_copy(0, way, sub).start()

        def forward(k, c):
            for way in range(2):
                x_arrival(k, way, sub - 1 - k).wait_recv()
                x_copy(k + 1, way, sub - 1 - k).start()
            return c

        lax.fori_loop(0, sub, forward, 0)
        lax.fori_loop(sub * rows_dev // SLICES, (sub + 1) * rows_dev // SLICES, tables, 0)
        return carry

    lax.fori_loop(0, SLICES, ramp, 0)

    for kind in range(base // 2, base):
        send_away(kind)
    owns[3].start()
    for w in range(3):
        owns[w].wait()
    for kind in range(base):
        held_copy(kind, partner, 0).wait_recv()

    def pass_part(p):
        for kind in range(3 * p, 3 * p + 3):
            for j in range(1, groups):
                owner = lax.rem(me_dp + n_dp - 2 * j, n_dp)
                held_copy(kind, owner, 0).wait_recv()
                held_copy(kind, owner, groups + j - 1).start()

    def rest_part(p):
        for kind in range(3 * p, 3 * p + 3):
            for i in range(1, groups):
                held_copy(kind, lax.rem(partner + 2 * i, n_dp), 0).wait_recv()

    second_own = (me_dp * width + out_columns(1, me_dp)) // chunk
    held = hop_of(second_own) == n_mp

    def send_second():
        for c in range(COLUMNS):
            send_away(base + COLUMNS + c)

    def project(way, g, u):
        halves = pl.ds(pl.multiple_of(way * half, 16), half)
        wide = xg[g, halves, pl.ds(pl.multiple_of(u * unit, 128), unit)].astype(jnp.float32)
        power = wide * wide
        total = power[:, 0:128]
        for i in range(1, unit // 128):
            total = total + power[:, i * 128:(i + 1) * 128]
        square[halves, :] += total
        start = g * chunk + u * unit
        scaled = (wide * gain_ref[:, pl.ds(pl.multiple_of(start, 128), unit)]).astype(jnp.bfloat16)
        acc[halves, :] += jnp.dot(
            scaled,
            wall[pl.ds(pl.multiple_of(start, 16), unit), :],
            preferred_element_type=jnp.float32,
        )

    def project_due(way, stage):
        def one(i, carry):
            hop = i // UNITS
            u = lax.rem(i, UNITS)
            g = ring_member(place + jnp.where(way == 0, -hop, hop), n_mp)
            start = g * chunk + u * unit
            owner = start // depth
            near = (owner // 2 == group) & ((start + unit - 1) // depth // 2 == group)
            if depth % unit == 0:
                needed = lax.rem(start + unit - 1, depth) // part_rows
            else:
                needed = PARTS - 1
            when = last
            for p in range(PARTS - 2, -1, -1):
                when = jnp.where(needed == p, part_stage[p], when)
            due = jnp.where(near, hop, jnp.maximum(hop, when))

            @pl.when(due == stage)
            def _():
                project(way, g, u)

            return carry

        lowest = jnp.where(stage >= part_stage[0], 0, stage)
        lax.fori_loop(lowest * UNITS, (stage + 1) * UNITS, one, 0)

    def stage_of(stage, carry):
        for p in range(PARTS):
            pl.when(stage == part_stage[p])(functools.partial(pass_part, p))

        def side(way, c):
            for i in range(SLICES // 2):
                sub = way * (SLICES // 2) + i
                for turn_way in range(2):

                    @pl.when((stage < last) & (stage + sub >= SLICES - 1))
                    def _():
                        x_arrival(stage, turn_way, sub).wait_recv()

                        @pl.when(stage < last - 1)
                        def _():
                            x_copy(stage + 1, turn_way, sub).start()

            for p in range(PARTS):
                pl.when((stage == part_stage[p]) & (way == 0))(functools.partial(rest_part, p))
            project_due(way, stage)
            return c

        lax.fori_loop(0, 2, side, 0)

        @pl.when(stage == 1)
        def _():
            for c in range(COLUMNS):
                send_away(base + c)

        @pl.when(stage == 2)
        def _():
            for kind in range(base, kinds):
                send_partner(kind)

        if n_out == 2:

            @pl.when((stage == 3) & jnp.logical_not(held))
            def _():
                send_second()

        return carry

    lax.fori_loop(0, n_mp, stage_of, 0)
    if n_out == 2:
        pl.when(held)(send_second)

    def turn(u, cosine, sine):
        return (u * cosine + pltpu.roll(u, HEAD_SIZE // 2, 1) * sine).astype(jnp.bfloat16)

    def attend(r, carry):
        rows = pl.ds(pl.multiple_of(r * ROW_TOKENS, ROW_TOKENS), ROW_TOKENS)
        power = jnp.sum(square[rows, :], axis=1, keepdims=True)
        scale = lax.rsqrt(power / (n_mp * chunk) + 1e-05)
        cosine = cos_ref[rows, :] * scale
        sine = sin_ref[rows, :] * scale
        seen = vis_ref[rows, :] > 0.5
        for kv in range(k_width // HEAD_SIZE):
            at_k = q_width + kv * HEAD_SIZE
            key = turn(acc[rows, at_k:at_k + HEAD_SIZE], cosine, sine)
            at_v = at_k + k_width
            value = (acc[rows, at_v:at_v + HEAD_SIZE] * scale).astype(jnp.bfloat16)
            heads = range(kv * QUERY_PER_KV, (kv + 1) * QUERY_PER_KV)
            queries = jnp.concatenate(
                [turn(acc[rows, h * HEAD_SIZE:(h + 1) * HEAD_SIZE], cosine, sine) for h in heads],
                axis=0,
            )
            scores = lax.dot_general(
                queries, key, (((1,), (1,)), ((), ())), preferred_element_type=jnp.float32
            ) * HEAD_SIZE ** (-0.5)
            probs = []
            for i in range(QUERY_PER_KV):
                own = scores[i * ROW_TOKENS:(i + 1) * ROW_TOKENS, :]
                own = jnp.where(seen, own, -1e30)
                expo = jnp.exp(own - jnp.max(own, axis=-1, keepdims=True))
                probs.append(
                    (expo / jnp.sum(expo, axis=-1, keepdims=True)).astype(jnp.bfloat16)
                )
            mixed = jnp.dot(
                jnp.concatenate(probs, axis=0), value, preferred_element_type=jnp.float32
            ).astype(jnp.bfloat16)
            for i, h in enumerate(heads):
                attn[rows, h * HEAD_SIZE:(h + 1) * HEAD_SIZE] = mixed[
                    i * ROW_TOKENS:(i + 1) * ROW_TOKENS, :
                ]
        return carry

    lax.fori_loop(0, tokens // ROW_TOKENS, attend, 0)
    owns[3].wait()

    if n_out == 1:
        for kind in range(base, kinds):
            for j in range(1, groups):
                owner = lax.rem(me_dp + n_dp - 2 * j, n_dp)
                held_copy(kind, owner, 0).wait_recv()
                held_copy(kind, owner, groups + j - 1).start()
            for i in range(groups):
                held_copy(kind, lax.rem(partner + 2 * i, n_dp), 0).wait_recv()

    def out_weights(g, c):
        return pl.ds(pl.multiple_of(g * chunk + c * column, 128), column)

    def need(g, c, way, hop):
        owner = g * chunk // width
        early = chunk * (hop_of(2 * owner + 1) < hop_of(2 * owner)).astype(jnp.int32)
        second = jnp.where(g * chunk - owner * width == early, 0, 1)
        kind = base + second * COLUMNS + c
        fresh = hop == hop_of(g)
        if way == 1:
            fresh = fresh & (2 * hop != n_mp) & (hop != n_mp)
        ref = wo.at[:, out_weights(g, c)]
        away = owner // 2 != group

        @pl.when(fresh & (lax.rem(owner, 2) == core) & away)
        def _():
            j = lax.rem(group - owner // 2 + groups, groups)
            weight_copy(kind, owner, ref, ref, 0, partner).wait_recv()
            weight_copy(kind, owner, ref, ref, groups + j - 1, partner).start()

        @pl.when(fresh & (lax.rem(owner, 2) != core))
        def _():
            weight_copy(kind, owner, ref, ref, 0, partner).wait_recv()

    def sum_copy(slot, way, c):
        cols = pl.ds(pl.multiple_of(c * column, 128), column)
        return pltpu.make_async_remote_copy(
            src_ref=sums.at[way, slot, :, cols],
            dst_ref=sums.at[way, slot + 1, :, cols],
            send_sem=s_send.at[way, c, slot],
            recv_sem=s_recv.at[way, c, slot],
            device_id={"mp": sides[way]},
            device_id_type=MESH,
        )

    def scatter(i, carry):
        hop = i // COLUMNS + 1
        c = lax.rem(i, COLUMNS)
        cols = pl.ds(pl.multiple_of(c * column, 128), column)
        for way in range(2):
            g = ring_member(place + (-hop if way == 0 else hop), n_mp)
            if n_out == 2:
                need(g, c, way, hop)
            terms[way] = jnp.dot(
                attn[way * half:(way + 1) * half, :],
                wo[:, out_weights(g, c)],
                preferred_element_type=jnp.float32,
            )
        for way in range(2):

            @pl.when(hop == 1)
            def _():
                sums[way, 0, :, cols] = terms[way].astype(jnp.bfloat16)

            @pl.when(hop > 1)
            def _():
                sum_copy(hop - 2, way, c).wait_recv()
                total = sums[way, hop - 1, :, cols].astype(jnp.float32) + terms[way]
                total = total.astype(jnp.bfloat16)

                @pl.when(hop < n_mp)
                def _():
                    sums[way, hop - 1, :, cols] = total

                @pl.when(hop == n_mp)
                def _():
                    out_ref[way * half:(way + 1) * half, cols] = total

            @pl.when(hop < n_mp)
            def _():
                sum_copy(hop - 1, way, c).start()

        return carry

    lax.fori_loop(0, n_mp * COLUMNS, scatter, 0)

    def drain(step, carry):
        for way in range(2):
            for sub in range(SLICES):
                x_copy(step, way, sub).wait_send()
            for c in range(COLUMNS):
                sum_copy(step, way, c).wait_send()
        return carry

    lax.fori_loop(0, n_mp - 1, drain, 0)
    for sub in range(SLICES):
        for j in range(1, n_dp):
            token_copy(j, sub, me_dp).wait_send()
    for kind in range(kinds):
        for i in range(2 * groups - 1):
            weight_copy(kind, me_dp, shard(kind), part(kind, me_dp), i, partner).wait_send()


def local(
    pair_tokens,
    norm_gain,
    q_weight,
    k_weight,
    value_weight,
    o_weight,
    pair_row,
    pair_span,
    block_ids,
):
    dp_count = lax.axis_size("dp")
    mp_count = lax.axis_size("mp")
    pairs_dev, pair_cap, width_local = pair_tokens.shape
    slots = dp_count * (-(-pairs_dev // dp_count))
    tok_dev = block_ids.shape[0]
    half = HEAD_SIZE // 2
    freq = 500000.0 ** (-(np.arange(half, dtype=np.float32) * 2.0 / HEAD_SIZE))
    freq = np.concatenate([freq, freq])[None, :].astype(np.float32)

    q_width = q_weight.shape[1]
    k_width = k_weight.shape[1]
    width = norm_gain.shape[0]
    n_out = pieces_of_output(mp_count, o_weight.shape[1], width_local)
    kinds = 3 * PARTS + n_out * COLUMNS
    far = dp_count - 1
    vmem = pl.BlockSpec(memory_space=pltpu.VMEM)
    smem = pl.BlockSpec(memory_space=pltpu.SMEM)
    anyspace = pl.BlockSpec(memory_space=pl.ANY)
    bf16 = jnp.bfloat16
    return pl.pallas_call(
        functools.partial(kernel, dp_count, mp_count),
        out_shape=jax.ShapeDtypeStruct((tok_dev, width_local), bf16),
        in_specs=[
            smem, smem, anyspace, vmem, anyspace, anyspace, anyspace, anyspace, vmem, vmem
        ],
        out_specs=vmem,
        scratch_shapes=[
            pltpu.VMEM((pairs_dev, pair_cap, width_local), bf16),
            pltpu.VMEM((slots * pair_cap, width_local), bf16),
            pltpu.VMEM((slots * pair_cap, width_local), bf16),
            pltpu.VMEM((mp_count, tok_dev, width_local), bf16),
            pltpu.VMEM((width, q_width + 2 * k_width), bf16),
            pltpu.VMEM((o_weight.shape[0], width), bf16),
            pltpu.VMEM((tok_dev, q_width + 2 * k_width), jnp.float32),
            pltpu.VMEM((tok_dev, 128), jnp.float32),
            pltpu.VMEM((tok_dev, q_width), bf16),
            pltpu.VMEM((2, mp_count, tok_dev // 2, width_local), bf16),
            pltpu.VMEM((2, tok_dev // 2, width_local // COLUMNS), jnp.float32),
            pltpu.VMEM((tok_dev, HEAD_SIZE), jnp.float32),
            pltpu.VMEM((tok_dev, HEAD_SIZE), jnp.float32),
            pltpu.VMEM((tok_dev, ROW_TOKENS), jnp.float32),
            pltpu.VMEM((tok_dev, slots * pair_cap), bf16),
            pltpu.SMEM((slots,), jnp.int32),
            pltpu.SMEM((slots,), jnp.int32),
            pltpu.SMEM((slots,), jnp.int32),
            pltpu.SemaphoreType.DMA((5,)),
            pltpu.SemaphoreType.DMA((SLICES, far)),
            pltpu.SemaphoreType.DMA((SLICES, dp_count)),
            pltpu.SemaphoreType.DMA((kinds, far)),
            pltpu.SemaphoreType.DMA((kinds, dp_count)),
            pltpu.SemaphoreType.DMA((2, SLICES, mp_count - 1)),
            pltpu.SemaphoreType.DMA((2, SLICES, mp_count - 1)),
            pltpu.SemaphoreType.DMA((2, COLUMNS, mp_count - 1)),
            pltpu.SemaphoreType.DMA((2, COLUMNS, mp_count - 1)),
        ],
        compiler_params=pltpu.CompilerParams(
            collective_id=0, has_side_effects=True, vmem_limit_bytes=60 * 1024 * 1024
        ),
    )(
        pair_row,
        pair_span,
        pair_tokens,
        norm_gain[None, :],
        q_weight,
        k_weight,
        value_weight,
        o_weight,
        block_ids.reshape(tok_dev // ROW_TOKENS, ROW_TOKENS),
        jnp.asarray(freq),
    )


def solution(mesh):
    placed = (
        P("dp", None, "mp"),
        P(),
        P("dp", "mp"),
        P("dp", "mp"),
        P("dp", "mp"),
        P("mp", "dp"),
        P(),
        P(),
        P("dp"),
    )
    return jax.shard_map(
        local, mesh=mesh, in_specs=placed, out_specs=P("dp", "mp"), check_vma=False
    )
```

time: 218 us -> 206 us (0.945)
  Pallas kernels: 206 us -> 199 us
  matrix products: 2.54 us -> 0 us
    pallas_call x1, Pallas kernels: 206 us -> 199 us  [local(): pl.pallas_call(functools.partial(kernel, dp_count, mp_count), out_shape=j...]
    dot_general x1 -> x0, matrix products: 2.54 us -> none  [local(): jnp.dot(pick, pair_tokens.reshape(pairs_dev * pair_cap, width_local), pre...]
where the time goes in v1:
time: 206 us; the launch traced here: 202 us
  Pallas kernels  199 us (97%)
  local copies, waits for them, and re-layouts  3.64 us (2%)
    pallas_call x1, Pallas kernels, local(): pl.pallas_call(functools.partial(kernel, dp_count, mp_count), out_shape=j...  199 us

profile of v1, /device:TPU:15, one launch (start us, length us, event | category | flops | bytes accessed | tf_op | source)
XLA Modules:
  0.0 202.3 jit_solution(1397003135062301354)
XLA Ops:
  0.0 1.4 copy.11.span_ref
  1.4 198.6 %shard_map.100 = bf16[512,1024]{1,0:T(8,128)(2,1)} custom-call(s32[64]{0:T(128)} %row_ref.1, s32[64,2]{1,0:T(8,128)} %copy.11.span_ref, bf16[16,48,1024]{2,1,0:T(8,128)(2,1)} %tok_ref.1, f32[1,8192]{1,0:T(1,128)} %bitcast.2, bf16[2048,512]{1,0:T(8,128)(2,1)} %q_ref.1, bf16[2048,128]{1,0:T(8,128)(2,1)} %k_ref.1, bf16[2048,128]{1,0:T(8,128)(2,1)} %v_ref.1, ...), custom_call_target="tpu_custom_call" | custom-call | tf_op jit(solution)/shard_map/pallas_call | solution.py:602
  200.0 2.3 %copy.13 = bf16[512,1024]{1,0:T(8,128)(2,1)} copy(bf16[512,1024]{1,0:T(8,128)(2,1)} %shard_map.100) | data formatting | bytes 2097152

commit v2 on v1

--- a/solution.py
+++ b/solution.py
@@ -23,12 +23,22 @@
     return jnp.where(place < count // 2, 2 * place, 2 * (count - 1 - place) + 1)
 
 
-def pieces_of_output(n_mp, width, chunk):
-    if width != 2 * chunk:
-        return 1
-    order = list(range(0, n_mp, 2)) + list(range(1, n_mp, 2))[::-1]
-    apart = all(order[p - 1] // 2 != order[(p + 1) % n_mp] // 2 for p in range(n_mp))
-    return 2 if apart else 1
+def pairs_up(n_dp, n_mp, width, chunk):
+    return n_dp // 2 == 2 and n_mp == 2 * n_dp and width == 2 * chunk
+
+
+def line_plan(length, group, at):
+    near = (2 * group, 2 * group + 1)
+    rising = list(range(length - 1, 0, -1))
+    if 1 in near:
+        rising = [1] + rising[:-1]
+    falling = list(range(length - 1))
+    if length - 2 in near:
+        falling = [length - 2] + falling[:-1]
+    units = [(rising.index(z), 0, z) for z in range(at + 1, length)]
+    units = sorted(units + [(falling.index(z), 1, z) for z in range(at)])
+    ties = [i for i in range(length - 2) if units[i][0] == units[i + 1][0]]
+    return [u[1] for u in units], [u[2] for u in units], (ties + [length])[0]
 
 
 def kernel(
@@ -38,6 +48,7 @@
     tokv, xout, xin, xg, wall, wo, acc, square, attn, sums, terms, cos_ref, sin_ref, vis_ref,
     put_ref, pick, first_of, length_of,
     own_sem, t_send, t_recv, w_send, w_recv, x_send, x_recv, s_send, s_recv,
+    b_send, b_recv, a_send, a_recv,
 ):
     me_dp = lax.axis_index("dp")
     me_mp = lax.axis_index("mp")
@@ -62,14 +73,23 @@
     depth, q_width = q_ref.shape
     k_width = k_ref.shape[1]
     width = o_ref.shape[1]
-    n_out = pieces_of_output(n_mp, width, chunk)
+    paired = pairs_up(n_dp, n_mp, width, chunk)
     slice_width = chunk // SLICES
     part_rows = depth // PARTS
     unit = chunk // UNITS
     column = chunk // COLUMNS
-    out_column = width // n_out // COLUMNS
+    out_column = width // COLUMNS
     base = 3 * PARTS
-    kinds = base + n_out * COLUMNS
+    kinds = base + (3 if paired else COLUMNS)
+    out_rows = o_ref.shape[0]
+    wide_half = chunk // 2
+    line = n_mp // 2
+    at_z = me_mp // 2
+    at_x = lax.rem(me_mp, 2)
+    mate = me_mp + 1 - 2 * at_x
+    inner = (at_z > 0) & (at_z < line - 1)
+    lead = jnp.where(at_z == 0, 1, jnp.where(at_z == line - 1, 0, group))
+    urgent = core == lead
     last = n_mp - 1
     part_stage = [min(2, last), min(4, last), min(5, last), last]
 
@@ -85,6 +105,22 @@
     for j in range(1, n_dp):
         peer = lax.rem(me_dp + j, n_dp)
         pl.semaphore_signal(barrier, inc=1, device_id={"dp": peer}, device_id_type=MESH)
+
+    greeted = 2 + n_dp - 1
+    if paired:
+        pl.semaphore_signal(barrier, inc=1, device_id={"mp": mate}, device_id_type=MESH)
+
+        @pl.when(at_z < line - 1)
+        def _():
+            above = jnp.minimum(me_mp + 2, n_mp - 1)
+            pl.semaphore_signal(barrier, inc=1, device_id={"mp": above}, device_id_type=MESH)
+
+        @pl.when(at_z > 0)
+        def _():
+            below = jnp.maximum(me_mp - 2, 0)
+            pl.semaphore_signal(barrier, inc=1, device_id={"mp": below}, device_id_type=MESH)
+
+        greeted = greeted + 1 + jnp.where(at_z < line - 1, 1, 0) + jnp.where(at_z > 0, 1, 0)
 
     owner_list = [lax.div(row_ref[me_dp * pairs_dev + p], rows_dev) for p in range(pairs_dev)]
     slot_list = []
@@ -99,7 +135,7 @@
             index = jnp.where(slot_list[p] == s, p, index)
         pick[s] = index
 
-    pl.semaphore_wait(barrier, 2 + n_dp - 1)
+    pl.semaphore_wait(barrier, greeted)
 
     def token_rows(owner):
         return pl.ds(pl.multiple_of(owner * block, 16), block)
@@ -130,24 +166,22 @@
     own_tokens.wait()
     lax.fori_loop(0, SLICES, send_tokens, 0)
 
-    def hop_of(g):
-        gap = lax.rem(place_of(g) - place + n_mp, n_mp)
-        gap = jnp.where(gap == 0, n_mp, gap)
-        return jnp.minimum(gap, jnp.where(gap == n_mp, n_mp, n_mp - gap))
-
-    def out_columns(second, owner):
-        if n_out == 1:
-            return owner * 0
-        later = (hop_of(2 * owner + 1) < hop_of(2 * owner)).astype(jnp.int32)
-        return chunk * (1 - later if second else later)
-
     starts = (0, q_width, q_width + k_width)
     spans = (q_width, k_width, k_width)
 
+    def pair_part(piece, owner):
+        side = at_x if piece == 0 else 1 - at_x
+        start = owner * chunk + max(piece - 1, 0) * wide_half
+        return wo.at[
+            pl.ds(pl.multiple_of(side * out_rows, 16), out_rows),
+            pl.ds(pl.multiple_of(start, 128), chunk if piece == 0 else wide_half),
+        ]
+
     def part(kind, owner):
+        if kind >= base and paired:
+            return pair_part(kind - base, owner)
         if kind >= base:
-            second, c = divmod(kind - base, COLUMNS)
-            start = owner * width + out_columns(second, owner) + c * out_column
+            start = owner * width + (kind - base) * out_column
             return wo.at[:, pl.ds(pl.multiple_of(start, 128), out_column)]
         p, which = divmod(kind, 3)
         start = owner * depth + p * part_rows
@@ -156,10 +190,12 @@
         ]
 
     def shard(kind):
+        if kind >= base and paired:
+            if kind > base:
+                return pair_part(kind - base, me_dp)
+            return o_ref.at[:, pl.ds(pl.multiple_of(at_x * chunk, 128), chunk)]
         if kind >= base:
-            second, c = divmod(kind - base, COLUMNS)
-            start = out_columns(second, me_dp) + c * out_column
-            return o_ref.at[:, pl.ds(pl.multiple_of(start, 128), out_column)]
+            return o_ref.at[:, pl.ds((kind - base) * out_column, out_column)]
         p, which = divmod(kind, 3)
         return (q_ref, k_ref, v_ref)[which].at[pl.ds(p * part_rows, part_rows), :]
 
@@ -193,13 +229,44 @@
         )
         for w in range(3)
     ]
-    owns.append(
-        pltpu.make_async_copy(
-            o_ref,
-            wo.at[:, pl.ds(pl.multiple_of(me_dp * width, 128), width)],
-            own_sem.at[3],
-        )
-    )
+    if paired:
+        owns.append(pltpu.make_async_copy(shard(base), part(base, me_dp), own_sem.at[3]))
+    else:
+        owns.append(
+            pltpu.make_async_copy(
+                o_ref,
+                wo.at[:, pl.ds(pl.multiple_of(me_dp * width, 128), width)],
+                own_sem.at[3],
+            )
+        )
+
+    def mate_copy(h, side):
+        start = me_dp * chunk + h * wide_half
+        taken = (1 - at_x) * chunk + h * wide_half
+        return pltpu.make_async_remote_copy(
+            src_ref=o_ref.at[:, pl.ds(pl.multiple_of(taken, 128), wide_half)],
+            dst_ref=wo.at[
+                pl.ds(pl.multiple_of(side * out_rows, 16), out_rows),
+                pl.ds(pl.multiple_of(start, 128), wide_half),
+            ],
+            send_sem=b_send.at[h],
+            recv_sem=b_recv.at[h],
+            device_id={"mp": mate},
+            device_id_type=MESH,
+        )
+
+    def mate_arrived():
+        for h in range(2):
+            mate_copy(h, 1 - at_x).wait_recv()
+            send_partner(base + 1 + h)
+
+    def mate_away():
+        for h in range(2):
+            send_away(base + 1 + h)
+
+    if paired:
+        pl.when(inner | urgent)(mate_copy(0, at_x).start)
+        pl.when(inner)(mate_copy(1, at_x).start)
 
     for kind in range(base // 2):
         send_away(kind)
@@ -241,8 +308,8 @@
         for p in range(pairs_dev):
             i = j * pairs_dev + p
             row = row_ref[i]
-            begin = span_ref[i, 0]
-            end = span_ref[i, 1]
+            begin = span_ref[0, i]
+            end = span_ref[1, i]
             first = lax.rem(row, rows_dev) * ROW_TOKENS + begin
             spot = jnp.where(lax.div(row, rows_dev) == me_dp, found, most)
             for k in range(most):
@@ -328,13 +395,6 @@
         for kind in range(3 * p, 3 * p + 3):
             for i in range(1, groups):
                 held_copy(kind, lax.rem(partner + 2 * i, n_dp), 0).wait_recv()
-
-    second_own = (me_dp * width + out_columns(1, me_dp)) // chunk
-    held = hop_of(second_own) == n_mp
-
-    def send_second():
-        for c in range(COLUMNS):
-            send_away(base + COLUMNS + c)
 
     def project(way, g, u):
         halves = pl.ds(pl.multiple_of(way * half, 16), half)
@@ -402,30 +462,51 @@
 
         lax.fori_loop(0, 2, side, 0)
 
-        @pl.when(stage == 1)
-        def _():
-            for c in range(COLUMNS):
-                send_away(base + c)
-
-        @pl.when(stage == 2)
-        def _():
-            for kind in range(base, kinds):
-                send_partner(kind)
-
-        if n_out == 2:
-
-            @pl.when((stage == 3) & jnp.logical_not(held))
-            def _():
-                send_second()
+        if paired:
+
+            @pl.when((stage == 1) & urgent)
+            def _():
+                send_away(base)
+
+            @pl.when(stage == 2)
+            def _():
+                send_partner(base)
+
+            @pl.when((stage == min(3, last)) & inner)
+            def _():
+                mate_arrived()
+                pl.when(urgent)(mate_away)
+
+        else:
+
+            @pl.when(stage == min(1, last))
+            def _():
+                for kind in range(base, kinds):
+                    send_away(kind)
+                    send_partner(kind)
 
         return carry
 
     lax.fori_loop(0, n_mp, stage_of, 0)
-    if n_out == 2:
-        pl.when(held)(send_second)
+    if paired:
+        pl.when(jnp.logical_not(inner) & urgent)(mate_copy(1, at_x).start)
 
     def turn(u, cosine, sine):
         return (u * cosine + pltpu.roll(u, HEAD_SIZE // 2, 1) * sine).astype(jnp.bfloat16)
+
+    def share(r, side):
+        ref = attn.at[
+            pl.ds(pl.multiple_of(r * ROW_TOKENS, ROW_TOKENS), ROW_TOKENS),
+            pl.ds(pl.multiple_of(side * q_width, 128), q_width),
+        ]
+        return pltpu.make_async_remote_copy(
+            src_ref=ref,
+            dst_ref=ref,
+            send_sem=a_send.at[r],
+            recv_sem=a_recv.at[r],
+            device_id={"mp": mate},
+            device_id_type=MESH,
+        )
 
     def attend(r, carry):
         rows = pl.ds(pl.multiple_of(r * ROW_TOKENS, ROW_TOKENS), ROW_TOKENS)
@@ -434,6 +515,7 @@
         cosine = cos_ref[rows, :] * scale
         sine = sin_ref[rows, :] * scale
         seen = vis_ref[rows, :] > 0.5
+        left = at_x * q_width if paired else 0
         for kv in range(k_width // HEAD_SIZE):
             at_k = q_width + kv * HEAD_SIZE
             key = turn(acc[rows, at_k:at_k + HEAD_SIZE], cosine, sine)
@@ -459,46 +541,136 @@
                 jnp.concatenate(probs, axis=0), value, preferred_element_type=jnp.float32
             ).astype(jnp.bfloat16)
             for i, h in enumerate(heads):
-                attn[rows, h * HEAD_SIZE:(h + 1) * HEAD_SIZE] = mixed[
-                    i * ROW_TOKENS:(i + 1) * ROW_TOKENS, :
-                ]
+                spot = pl.ds(pl.multiple_of(left + h * HEAD_SIZE, 128), HEAD_SIZE)
+                attn[rows, spot] = mixed[i * ROW_TOKENS:(i + 1) * ROW_TOKENS, :]
+        if paired:
+            share(r, at_x).start()
         return carry
 
     lax.fori_loop(0, tokens // ROW_TOKENS, attend, 0)
     owns[3].wait()
 
-    if n_out == 1:
-        for kind in range(base, kinds):
-            for j in range(1, groups):
-                owner = lax.rem(me_dp + n_dp - 2 * j, n_dp)
-                held_copy(kind, owner, 0).wait_recv()
-                held_copy(kind, owner, groups + j - 1).start()
-            for i in range(groups):
-                held_copy(kind, lax.rem(partner + 2 * i, n_dp), 0).wait_recv()
-
-    def out_weights(g, c):
-        return pl.ds(pl.multiple_of(g * chunk + c * column, 128), column)
-
-    def need(g, c, way, hop):
-        owner = g * chunk // width
-        early = chunk * (hop_of(2 * owner + 1) < hop_of(2 * owner)).astype(jnp.int32)
-        second = jnp.where(g * chunk - owner * width == early, 0, 1)
-        kind = base + second * COLUMNS + c
-        fresh = hop == hop_of(g)
-        if way == 1:
-            fresh = fresh & (2 * hop != n_mp) & (hop != n_mp)
-        ref = wo.at[:, out_weights(g, c)]
-        away = owner // 2 != group
-
-        @pl.when(fresh & (lax.rem(owner, 2) == core) & away)
+    def line_copy(way, z, r):
+        ref = sums.at[way, z, pl.ds(pl.multiple_of(r * ROW_TOKENS, ROW_TOKENS), ROW_TOKENS), :]
+        ahead = jnp.clip(me_mp + 2 - 4 * way, 0, n_mp - 1)
+        return pltpu.make_async_remote_copy(
+            src_ref=ref,
+            dst_ref=ref,
+            send_sem=s_send.at[way, z, r],
+            recv_sem=s_recv.at[way, z, r],
+            device_id={"mp": ahead},
+            device_id_type=MESH,
+        )
+
+    def need(z):
+        away = z // 2 != group
+
+        @pl.when(z == partner)
         def _():
-            j = lax.rem(group - owner // 2 + groups, groups)
-            weight_copy(kind, owner, ref, ref, 0, partner).wait_recv()
-            weight_copy(kind, owner, ref, ref, groups + j - 1, partner).start()
-
-        @pl.when(fresh & (lax.rem(owner, 2) != core))
+            for piece in range(3):
+                ref = pair_part(piece, z)
+                weight_copy(base + piece, z, ref, ref, 0, partner).wait_recv()
+
+        @pl.when(away & (lax.rem(z, 2) == core))
         def _():
-            weight_copy(kind, owner, ref, ref, 0, partner).wait_recv()
+            for piece in range(3):
+                ref = pair_part(piece, z)
+                weight_copy(base + piece, z, ref, ref, 0, partner).wait_recv()
+                weight_copy(base + piece, z, ref, ref, groups, partner).start()
+
+        @pl.when(away & (lax.rem(z, 2) != core))
+        def _():
+            for piece in range(3):
+                ref = pair_part(piece, z)
+                weight_copy(base + piece, z, ref, ref, 0, partner).wait_recv()
+
+    def along_line():
+        pl.when(jnp.logical_not(inner | urgent))(mate_copy(0, at_x).start)
+        pl.when(jnp.logical_not(inner | urgent))(mate_copy(1, at_x).start)
+        pl.when(jnp.logical_not(urgent))(functools.partial(send_away, base))
+
+        @pl.when(jnp.logical_not(inner) & urgent)
+        def _():
+            mate_arrived()
+            mate_away()
+
+        units = line - 1
+        ways = [jnp.int32(0)] * units
+        ends = [jnp.int32(0)] * units
+        tie = jnp.int32(line)
+        for plane in range(groups):
+            for z in range(line):
+                plan = line_plan(line, plane, z)
+                here = (group == plane) & (at_z == z)
+                for i in range(units):
+                    ways[i] = jnp.where(here, plan[0][i], ways[i])
+                    ends[i] = jnp.where(here, plan[1][i], ends[i])
+                tie = jnp.where(here, plan[2], tie)
+
+        def entry(i, carry):
+            @pl.when((i == rows_dev) & jnp.logical_not(urgent))
+            def _():
+                pl.when(jnp.logical_not(inner))(mate_arrived)
+                mate_away()
+
+            within = i - tie * rows_dev
+            mixed = (within >= 0) & (within < 2 * rows_dev)
+            u = jnp.where(mixed, tie + lax.rem(within, 2), i // rows_dev)
+            r = jnp.where(mixed, within // 2, lax.rem(i, rows_dev))
+            own = u == units
+            way = jnp.int32(0)
+            z = at_z
+            for k in range(units):
+                way = jnp.where(u == k, ways[k], way)
+                z = jnp.where(u == k, ends[k], z)
+            rows = pl.ds(pl.multiple_of(r * ROW_TOKENS, ROW_TOKENS), ROW_TOKENS)
+
+            pl.when(r == 0)(functools.partial(need, z))
+
+            @pl.when(u == 0)
+            def _():
+                share(r, 1 - at_x).wait_recv()
+
+            terms[...] = jnp.dot(
+                attn[rows, :],
+                wo[:, pl.ds(pl.multiple_of(z * chunk, 128), chunk)],
+                preferred_element_type=jnp.float32,
+            )
+            for side in range(2):
+                more = at_z > 0 if side == 0 else at_z < line - 1
+
+                @pl.when(more & (own | (way == side)))
+                def _():
+                    line_copy(side, z, r).wait_recv()
+                    terms[...] += sums[side, z, rows, :].astype(jnp.float32)
+
+            @pl.when(own)
+            def _():
+                out_ref[rows, :] = terms[...].astype(jnp.bfloat16)
+
+            for side in range(2):
+
+                @pl.when(jnp.logical_not(own) & (way == side))
+                def _():
+                    sums[side, z, rows, :] = terms[...].astype(jnp.bfloat16)
+                    line_copy(side, z, r).start()
+
+            return carry
+
+        lax.fori_loop(0, line * rows_dev, entry, 0)
+
+        def sent(i, carry):
+            z = i // rows_dev
+            r = lax.rem(i, rows_dev)
+            pl.when(z > at_z)(line_copy(0, z, r).wait_send)
+            pl.when(z < at_z)(line_copy(1, z, r).wait_send)
+            return carry
+
+        lax.fori_loop(0, line * rows_dev, sent, 0)
+        for h in range(2):
+            mate_copy(h, at_x).wait_send()
+        for r in range(rows_dev):
+            share(r, at_x).wait_send()
 
     def sum_copy(slot, way, c):
         cols = pl.ds(pl.multiple_of(c * column, 128), column)
@@ -517,11 +689,9 @@
         cols = pl.ds(pl.multiple_of(c * column, 128), column)
         for way in range(2):
             g = ring_member(place + (-hop if way == 0 else hop), n_mp)
-            if n_out == 2:
-                need(g, c, way, hop)
             terms[way] = jnp.dot(
                 attn[way * half:(way + 1) * half, :],
-                wo[:, out_weights(g, c)],
+                wo[:, pl.ds(pl.multiple_of(g * chunk + c * column, 128), column)],
                 preferred_element_type=jnp.float32,
             )
         for way in range(2):
@@ -550,14 +720,33 @@
 
         return carry
 
-    lax.fori_loop(0, n_mp * COLUMNS, scatter, 0)
+    def around_ring():
+        for kind in range(base, kinds):
+            for j in range(1, groups):
+                owner = lax.rem(me_dp + n_dp - 2 * j, n_dp)
+                held_copy(kind, owner, 0).wait_recv()
+                held_copy(kind, owner, groups + j - 1).start()
+            for i in range(groups):
+                held_copy(kind, lax.rem(partner + 2 * i, n_dp), 0).wait_recv()
+        lax.fori_loop(0, n_mp * COLUMNS, scatter, 0)
+
+        def sent(step, carry):
+            for way in range(2):
+                for c in range(COLUMNS):
+                    sum_copy(step, way, c).wait_send()
+            return carry
+
+        lax.fori_loop(0, n_mp - 1, sent, 0)
+
+    if paired:
+        along_line()
+    else:
+        around_ring()
 
     def drain(step, carry):
         for way in range(2):
             for sub in range(SLICES):
                 x_copy(step, way, sub).wait_send()
-            for c in range(COLUMNS):
-                sum_copy(step, way, c).wait_send()
         return carry
 
     lax.fori_loop(0, n_mp - 1, drain, 0)
@@ -592,8 +781,22 @@
     q_width = q_weight.shape[1]
     k_width = k_weight.shape[1]
     width = norm_gain.shape[0]
-    n_out = pieces_of_output(mp_count, o_weight.shape[1], width_local)
-    kinds = 3 * PARTS + n_out * COLUMNS
+    out_rows = o_weight.shape[0]
+    if pairs_up(dp_count, mp_count, o_weight.shape[1], width_local):
+        kinds = 3 * PARTS + 3
+        line = mp_count // 2
+        attn_shape = (tok_dev, 2 * q_width)
+        wo_shape = (2 * out_rows, width // 2)
+        sums_shape = (2, line, tok_dev, width_local)
+        terms_shape = (ROW_TOKENS, width_local)
+        sum_sems = (2, line, tok_dev // ROW_TOKENS)
+    else:
+        kinds = 3 * PARTS + COLUMNS
+        attn_shape = (tok_dev, q_width)
+        wo_shape = (out_rows, width)
+        sums_shape = (2, mp_count, tok_dev // 2, width_local)
+        terms_shape = (2, tok_dev // 2, width_local // COLUMNS)
+        sum_sems = (2, COLUMNS, mp_count - 1)
     far = dp_count - 1
     vmem = pl.BlockSpec(memory_space=pltpu.VMEM)
     smem = pl.BlockSpec(memory_space=pltpu.SMEM)
@@ -612,12 +815,12 @@
             pltpu.VMEM((slots * pair_cap, width_local), bf16),
             pltpu.VMEM((mp_count, tok_dev, width_local), bf16),
             pltpu.VMEM((width, q_width + 2 * k_width), bf16),
-            pltpu.VMEM((o_weight.shape[0], width), bf16),
+            pltpu.VMEM(wo_shape, bf16),
             pltpu.VMEM((tok_dev, q_width + 2 * k_width), jnp.float32),
             pltpu.VMEM((tok_dev, 128), jnp.float32),
-            pltpu.VMEM((tok_dev, q_width), bf16),
-            pltpu.VMEM((2, mp_count, tok_dev // 2, width_local), bf16),
-            pltpu.VMEM((2, tok_dev // 2, width_local // COLUMNS), jnp.float32),
+            pltpu.VMEM(attn_shape, bf16),
+            pltpu.VMEM(sums_shape, bf16),
+            pltpu.VMEM(terms_shape, jnp.float32),
             pltpu.VMEM((tok_dev, HEAD_SIZE), jnp.float32),
             pltpu.VMEM((tok_dev, HEAD_SIZE), jnp.float32),
             pltpu.VMEM((tok_dev, ROW_TOKENS), jnp.float32),
@@ -632,15 +835,19 @@
             pltpu.SemaphoreType.DMA((kinds, dp_count)),
             pltpu.SemaphoreType.DMA((2, SLICES, mp_count - 1)),
             pltpu.SemaphoreType.DMA((2, SLICES, mp_count - 1)),
-            pltpu.SemaphoreType.DMA((2, COLUMNS, mp_count - 1)),
-            pltpu.SemaphoreType.DMA((2, COLUMNS, mp_count - 1)),
+            pltpu.SemaphoreType.DMA(sum_sems),
+            pltpu.SemaphoreType.DMA(sum_sems),
+            pltpu.SemaphoreType.DMA((2,)),
+            pltpu.SemaphoreType.DMA((2,)),
+            pltpu.SemaphoreType.DMA((tok_dev // ROW_TOKENS,)),
+            pltpu.SemaphoreType.DMA((tok_dev // ROW_TOKENS,)),
         ],
         compiler_params=pltpu.CompilerParams(
             collective_id=0, has_side_effects=True, vmem_limit_bytes=60 * 1024 * 1024
         ),
     )(
         pair_row,
-        pair_span,
+        jnp.transpose(pair_span),
         pair_tokens,
         norm_gain[None, :],
         q_weight,

time: 206 us -> 201 us (0.976); the launches traced: 202 us -> 201 us
  no operation moved by 1% of the time
where the time goes in v2:
time: 201 us
  Pallas kernels  199 us (99%)
  local copies, waits for them, and re-layouts  2.26 us (1%)
    pallas_call x1, Pallas kernels, local(): pl.pallas_call(functools.partial(kernel, dp_count, mp_count), out_shape=j...  199 us

profile of v2, /device:TPU:15, one launch (start us, length us, event | category | flops | bytes accessed | tf_op | source)
XLA Modules:
  0.0 200.8 jit_solution(17606997363030005065)
XLA Ops:
  0.0 198.6 %shard_map.100 = bf16[512,1024]{1,0:T(8,128)(2,1)} custom-call(s32[64]{0:T(128)} %row_ref.1, s32[2,64]{1,0:T(2,128)} %bitcast.5, bf16[16,48,1024]{2,1,0:T(8,128)(2,1)} %tok_ref.1, f32[1,8192]{1,0:T(1,128)} %bitcast.3, bf16[2048,512]{1,0:T(8,128)(2,1)} %q_ref.1, bf16[2048,128]{1,0:T(8,128)(2,1)} %k_ref.1, bf16[2048,128]{1,0:T(8,128)(2,1)} %v_ref.1, ...), custom_call_target="tpu_custom_call" | custom-call | tf_op jit(solution)/shard_map/pallas_call | solution.py:805
  198.6 2.3 %copy.12 = bf16[512,1024]{1,0:T(8,128)(2,1)} copy(bf16[512,1024]{1,0:T(8,128)(2,1)} %shard_map.100) | data formatting | bytes 2097152

commit v3 on v2

--- a/solution.py
+++ b/solution.py
@@ -11,7 +11,7 @@
 HEAD_SIZE = 128
 ROW_TOKENS = 128
 QUERY_PER_KV = 4
-SLICES = 4
+SLICES = 2
 PARTS = 4
 COLUMNS = 4
 UNITS = 2
@@ -91,7 +91,8 @@
     lead = jnp.where(at_z == 0, 1, jnp.where(at_z == line - 1, 0, group))
     urgent = core == lead
     last = n_mp - 1
-    part_stage = [min(2, last), min(4, last), min(5, last), last]
+    final = 2 * last
+    part_slot = [min(2 * p, final - 1) for p in (2, 4, 6, n_mp)]
 
     def token_slice(sub):
         return pl.ds(pl.multiple_of(sub * slice_width, 128), slice_width)
@@ -255,18 +256,16 @@
             device_id_type=MESH,
         )
 
-    def mate_arrived():
+    def mate_arrived(h):
+        mate_copy(h, 1 - at_x).wait_recv()
+        send_partner(base + 1 + h)
+
+    def mate_away(h):
+        send_away(base + 1 + h)
+
+    if paired:
         for h in range(2):
-            mate_copy(h, 1 - at_x).wait_recv()
-            send_partner(base + 1 + h)
-
-    def mate_away():
-        for h in range(2):
-            send_away(base + 1 + h)
-
-    if paired:
-        pl.when(inner | urgent)(mate_copy(0, at_x).start)
-        pl.when(inner)(mate_copy(1, at_x).start)
+            pl.when(inner | urgent)(mate_copy(h, at_x).start)
 
     for kind in range(base // 2):
         send_away(kind)
@@ -370,7 +369,7 @@
                 x_copy(k + 1, way, sub - 1 - k).start()
             return c
 
-        lax.fori_loop(0, sub, forward, 0)
+        lax.fori_loop(0, jnp.minimum(sub, last - 1), forward, 0)
         lax.fori_loop(sub * rows_dev // SLICES, (sub + 1) * rows_dev // SLICES, tables, 0)
         return carry
 
@@ -412,10 +411,17 @@
             preferred_element_type=jnp.float32,
         )
 
-    def project_due(way, stage):
+    def project_due(slot):
+        stage = slot // 2
+        newest = jnp.minimum(stage + 1, last)
+        catch_up = slot == 0
+        for p in range(PARTS):
+            catch_up = catch_up | (slot == part_slot[p])
+
         def one(i, carry):
-            hop = i // UNITS
-            u = lax.rem(i, UNITS)
+            hop = i // (2 * UNITS)
+            u = lax.rem(i // 2, UNITS)
+            way = lax.rem(i, 2)
             g = ring_member(place + jnp.where(way == 0, -hop, hop), n_mp)
             start = g * chunk + u * unit
             owner = start // depth
@@ -424,62 +430,63 @@
                 needed = lax.rem(start + unit - 1, depth) // part_rows
             else:
                 needed = PARTS - 1
-            when = last
+            when = part_slot[PARTS - 1]
             for p in range(PARTS - 2, -1, -1):
-                when = jnp.where(needed == p, part_stage[p], when)
-            due = jnp.where(near, hop, jnp.maximum(hop, when))
-
-            @pl.when(due == stage)
+                when = jnp.where(needed == p, part_slot[p], when)
+            here = jnp.where(hop == 0, 0, 2 * (hop - 1) + u)
+            here = jnp.where(here == final - 1, final, here)
+            due = jnp.where(near, here, jnp.maximum(here, when))
+
+            @pl.when(due == slot)
             def _():
                 project(way, g, u)
 
             return carry
 
-        lowest = jnp.where(stage >= part_stage[0], 0, stage)
-        lax.fori_loop(lowest * UNITS, (stage + 1) * UNITS, one, 0)
-
-    def stage_of(stage, carry):
+        lowest = jnp.where(catch_up, 0, newest)
+        lax.fori_loop(lowest * 2 * UNITS, (newest + 1) * 2 * UNITS, one, 0)
+
+    def slot_of(slot, carry):
         for p in range(PARTS):
-            pl.when(stage == part_stage[p])(functools.partial(pass_part, p))
-
-        def side(way, c):
-            for i in range(SLICES // 2):
-                sub = way * (SLICES // 2) + i
-                for turn_way in range(2):
-
-                    @pl.when((stage < last) & (stage + sub >= SLICES - 1))
+            pl.when(slot == part_slot[p])(functools.partial(pass_part, p))
+        stage = jnp.minimum(slot // 2, last - 1)
+        side = jnp.where(slot == final, 1, lax.rem(slot, 2))
+        for i in range(SLICES // 2):
+            sub = side * (SLICES // 2) + i
+            for way in range(2):
+                fresh = (slot != final - 1) & ((stage + sub >= SLICES - 1) | (stage == last - 1))
+
+                @pl.when(fresh)
+                def _():
+                    x_arrival(stage, way, sub).wait_recv()
+
+                    @pl.when(stage < last - 1)
                     def _():
-                        x_arrival(stage, turn_way, sub).wait_recv()
-
-                        @pl.when(stage < last - 1)
-                        def _():
-                            x_copy(stage + 1, turn_way, sub).start()
-
-            for p in range(PARTS):
-                pl.when((stage == part_stage[p]) & (way == 0))(functools.partial(rest_part, p))
-            project_due(way, stage)
-            return c
-
-        lax.fori_loop(0, 2, side, 0)
+                        x_copy(stage + 1, way, sub).start()
+
+        for p in range(PARTS):
+            pl.when(slot == part_slot[p])(functools.partial(rest_part, p))
+        project_due(slot)
 
         if paired:
 
-            @pl.when((stage == 1) & urgent)
+            @pl.when((slot == 2) & urgent)
             def _():
                 send_away(base)
 
-            @pl.when(stage == 2)
+            @pl.when(slot == 3)
             def _():
                 send_partner(base)
 
-            @pl.when((stage == min(3, last)) & inner)
-            def _():
-                mate_arrived()
-                pl.when(urgent)(mate_away)
+            @pl.when(slot == min(6, final))
+            def _():
+                for h in range(2):
+                    pl.when(inner | urgent)(functools.partial(mate_arrived, h))
+                    pl.when(urgent)(functools.partial(mate_away, h))
 
         else:
 
-            @pl.when(stage == min(1, last))
+            @pl.when(slot == min(2, final))
             def _():
                 for kind in range(base, kinds):
                     send_away(kind)
@@ -487,10 +494,7 @@
 
         return carry
 
-    lax.fori_loop(0, n_mp, stage_of, 0)
-    if paired:
-        pl.when(jnp.logical_not(inner) & urgent)(mate_copy(1, at_x).start)
-
+    lax.fori_loop(0, final + 1, slot_of, 0)
     def turn(u, cosine, sine):
         return (u * cosine + pltpu.roll(u, HEAD_SIZE // 2, 1) * sine).astype(jnp.bfloat16)
 
@@ -551,7 +555,13 @@
     owns[3].wait()
 
     def line_copy(way, z, r):
-        ref = sums.at[way, z, pl.ds(pl.multiple_of(r * ROW_TOKENS, ROW_TOKENS), ROW_TOKENS), :]
+        h = r // rows_dev
+        ref = sums.at[
+            way,
+            z,
+            pl.ds(pl.multiple_of(lax.rem(r, rows_dev) * ROW_TOKENS, ROW_TOKENS), ROW_TOKENS),
+            pl.ds(pl.multiple_of(h * wide_half, 128), wide_half),
+        ]
         ahead = jnp.clip(me_mp + 2 - 4 * way, 0, n_mp - 1)
         return pltpu.make_async_remote_copy(
             src_ref=ref,
@@ -562,37 +572,35 @@
             device_id_type=MESH,
         )
 
-    def need(z):
+    def need(z, pieces):
         away = z // 2 != group
 
         @pl.when(z == partner)
         def _():
-            for piece in range(3):
+            for piece in pieces:
                 ref = pair_part(piece, z)
                 weight_copy(base + piece, z, ref, ref, 0, partner).wait_recv()
 
         @pl.when(away & (lax.rem(z, 2) == core))
         def _():
-            for piece in range(3):
+            for piece in pieces:
                 ref = pair_part(piece, z)
                 weight_copy(base + piece, z, ref, ref, 0, partner).wait_recv()
                 weight_copy(base + piece, z, ref, ref, groups, partner).start()
 
         @pl.when(away & (lax.rem(z, 2) != core))
         def _():
-            for piece in range(3):
+            for piece in pieces:
                 ref = pair_part(piece, z)
                 weight_copy(base + piece, z, ref, ref, 0, partner).wait_recv()
 
     def along_line():
-        pl.when(jnp.logical_not(inner | urgent))(mate_copy(0, at_x).start)
-        pl.when(jnp.logical_not(inner | urgent))(mate_copy(1, at_x).start)
-        pl.when(jnp.logical_not(urgent))(functools.partial(send_away, base))
-
-        @pl.when(jnp.logical_not(inner) & urgent)
-        def _():
-            mate_arrived()
-            mate_away()
+        outer = jnp.logical_not(inner)
+        lazy = jnp.logical_not(urgent)
+        for h in range(2):
+            pl.when(outer & lazy)(mate_copy(h, at_x).start)
+        pl.when(lazy)(functools.partial(send_away, base))
+        entries = 2 * rows_dev
 
         units = line - 1
         ways = [jnp.int32(0)] * units
@@ -608,15 +616,18 @@
                 tie = jnp.where(here, plan[2], tie)
 
         def entry(i, carry):
-            @pl.when((i == rows_dev) & jnp.logical_not(urgent))
-            def _():
-                pl.when(jnp.logical_not(inner))(mate_arrived)
-                mate_away()
-
-            within = i - tie * rows_dev
-            mixed = (within >= 0) & (within < 2 * rows_dev)
-            u = jnp.where(mixed, tie + lax.rem(within, 2), i // rows_dev)
-            r = jnp.where(mixed, within // 2, lax.rem(i, rows_dev))
+            @pl.when((i == entries) & lazy)
+            def _():
+                for h in range(2):
+                    pl.when(outer)(functools.partial(mate_arrived, h))
+                    mate_away(h)
+
+            within = i - tie * entries
+            mixed = (within >= 0) & (within < 2 * entries)
+            u = jnp.where(mixed, tie + lax.rem(within, 2), i // entries)
+            e = jnp.where(mixed, within // 2, lax.rem(i, entries))
+            h = e // rows_dev
+            r = lax.rem(e, rows_dev)
             own = u == units
             way = jnp.int32(0)
             z = at_z
@@ -625,15 +636,17 @@
                 z = jnp.where(u == k, ends[k], z)
             rows = pl.ds(pl.multiple_of(r * ROW_TOKENS, ROW_TOKENS), ROW_TOKENS)
 
-            pl.when(r == 0)(functools.partial(need, z))
-
-            @pl.when(u == 0)
+            cols = pl.ds(pl.multiple_of(h * wide_half, 128), wide_half)
+            pl.when(e == 0)(functools.partial(need, z, (0, 1)))
+            pl.when(e == rows_dev)(functools.partial(need, z, (2,)))
+
+            @pl.when((u == 0) & (h == 0))
             def _():
                 share(r, 1 - at_x).wait_recv()
 
             terms[...] = jnp.dot(
                 attn[rows, :],
-                wo[:, pl.ds(pl.multiple_of(z * chunk, 128), chunk)],
+                wo[:, pl.ds(pl.multiple_of(z * chunk + h * wide_half, 128), wide_half)],
                 preferred_element_type=jnp.float32,
             )
             for side in range(2):
@@ -641,32 +654,32 @@
 
                 @pl.when(more & (own | (way == side)))
                 def _():
-                    line_copy(side, z, r).wait_recv()
-                    terms[...] += sums[side, z, rows, :].astype(jnp.float32)
+                    line_copy(side, z, e).wait_recv()
+                    terms[...] += sums[side, z, rows, cols].astype(jnp.float32)
 
             @pl.when(own)
             def _():
-                out_ref[rows, :] = terms[...].astype(jnp.bfloat16)
+                out_ref[rows, cols] = terms[...].astype(jnp.bfloat16)
 
             for side in range(2):
 
                 @pl.when(jnp.logical_not(own) & (way == side))
                 def _():
-                    sums[side, z, rows, :] = terms[...].astype(jnp.bfloat16)
-                    line_copy(side, z, r).start()
+                    sums[side, z, rows, cols] = terms[...].astype(jnp.bfloat16)
+                    line_copy(side, z, e).start()
 
             return carry
 
-        lax.fori_loop(0, line * rows_dev, entry, 0)
+        lax.fori_loop(0, line * entries, entry, 0)
 
         def sent(i, carry):
-            z = i // rows_dev
-            r = lax.rem(i, rows_dev)
-            pl.when(z > at_z)(line_copy(0, z, r).wait_send)
-            pl.when(z < at_z)(line_copy(1, z, r).wait_send)
+            z = i // entries
+            e = lax.rem(i, entries)
+            pl.when(z > at_z)(line_copy(0, z, e).wait_send)
+            pl.when(z < at_z)(line_copy(1, z, e).wait_send)
             return carry
 
-        lax.fori_loop(0, line * rows_dev, sent, 0)
+        lax.fori_loop(0, line * entries, sent, 0)
         for h in range(2):
             mate_copy(h, at_x).wait_send()
         for r in range(rows_dev):
@@ -788,8 +801,8 @@
         attn_shape = (tok_dev, 2 * q_width)
         wo_shape = (2 * out_rows, width // 2)
         sums_shape = (2, line, tok_dev, width_local)
-        terms_shape = (ROW_TOKENS, width_local)
-        sum_sems = (2, line, tok_dev // ROW_TOKENS)
+        terms_shape = (ROW_TOKENS, width_local // 2)
+        sum_sems = (2, line, 2 * (tok_dev // ROW_TOKENS))
     else:
         kinds = 3 * PARTS + COLUMNS
         attn_shape = (tok_dev, q_width)
@@ -804,7 +817,7 @@
     bf16 = jnp.bfloat16
     return pl.pallas_call(
         functools.partial(kernel, dp_count, mp_count),
-        out_shape=jax.ShapeDtypeStruct((tok_dev, width_local), bf16),
+        out_shape=pltpu.VMEM((tok_dev, width_local), bf16),
         in_specs=[
             smem, smem, anyspace, vmem, anyspace, anyspace, anyspace, anyspace, vmem, vmem
         ],

time: 201 us -> 190 us (0.945)
  Pallas kernels: 199 us -> 188 us
    pallas_call x1, Pallas kernels: 199 us -> 188 us  [local(): pl.pallas_call(functools.partial(kernel, dp_count, mp_count), out_shape=p...]
where the time goes in v3:
time: 190 us; the launch traced here: 189 us
  Pallas kernels  188 us (99%)
    pallas_call x1, Pallas kernels, local(): pl.pallas_call(functools.partial(kernel, dp_count, mp_count), out_shape=p...  188 us

profile of v3, /device:TPU:15, one launch (start us, length us, event | category | flops | bytes accessed | tf_op | source)
XLA Modules:
  0.0 188.7 jit_solution(13901088423257686795)
XLA Ops:
  0.0 187.8 %shard_map.100 = bf16[512,1024]{1,0:T(8,128)(2,1)S(1)} custom-call(s32[64]{0:T(128)} %row_ref.1, s32[2,64]{1,0:T(2,128)} %bitcast.5, bf16[16,48,1024]{2,1,0:T(8,128)(2,1)} %tok_ref.1, f32[1,8192]{1,0:T(1,128)} %bitcast.3, bf16[2048,512]{1,0:T(8,128)(2,1)} %q_ref.1, bf16[2048,128]{1,0:T(8,128)(2,1)} %k_ref.1, bf16[2048,128]{1,0:T(8,128)(2,1)} %v_ref.1, ...), custom_call_target="tpu_custom_call" | custom-call | tf_op jit(solution)/shard_map/pallas_call | solution.py:818
  187.8 1.0 copy.12

commit v4 on v3

--- a/solution.py
+++ b/solution.py
@@ -12,8 +12,9 @@
 ROW_TOKENS = 128
 QUERY_PER_KV = 4
 SLICES = 2
-PARTS = 4
+PARTS = 2
 COLUMNS = 4
+LINE_COLUMNS = 1
 UNITS = 2
 MESH = pl.DeviceIdType.MESH
 
@@ -83,6 +84,7 @@
     kinds = base + (3 if paired else COLUMNS)
     out_rows = o_ref.shape[0]
     wide_half = chunk // 2
+    line_width = chunk // LINE_COLUMNS
     line = n_mp // 2
     at_z = me_mp // 2
     at_x = lax.rem(me_mp, 2)
@@ -92,7 +94,7 @@
     urgent = core == lead
     last = n_mp - 1
     final = 2 * last
-    part_slot = [min(2 * p, final - 1) for p in (2, 4, 6, n_mp)]
+    part_slot = [min(2 * p, final - 1) for p in (4, n_mp)]
 
     def token_slice(sub):
         return pl.ds(pl.multiple_of(sub * slice_width, 128), slice_width)
@@ -560,7 +562,7 @@
             way,
             z,
             pl.ds(pl.multiple_of(lax.rem(r, rows_dev) * ROW_TOKENS, ROW_TOKENS), ROW_TOKENS),
-            pl.ds(pl.multiple_of(h * wide_half, 128), wide_half),
+            pl.ds(pl.multiple_of(h * line_width, 128), line_width),
         ]
         ahead = jnp.clip(me_mp + 2 - 4 * way, 0, n_mp - 1)
         return pltpu.make_async_remote_copy(
@@ -600,7 +602,7 @@
         for h in range(2):
             pl.when(outer & lazy)(mate_copy(h, at_x).start)
         pl.when(lazy)(functools.partial(send_away, base))
-        entries = 2 * rows_dev
+        entries = LINE_COLUMNS * rows_dev
 
         units = line - 1
         ways = [jnp.int32(0)] * units
@@ -636,9 +638,11 @@
                 z = jnp.where(u == k, ends[k], z)
             rows = pl.ds(pl.multiple_of(r * ROW_TOKENS, ROW_TOKENS), ROW_TOKENS)
 
-            cols = pl.ds(pl.multiple_of(h * wide_half, 128), wide_half)
-            pl.when(e == 0)(functools.partial(need, z, (0, 1)))
-            pl.when(e == rows_dev)(functools.partial(need, z, (2,)))
+            cols = pl.ds(pl.multiple_of(h * line_width, 128), line_width)
+            pl.when(e == 0)(functools.partial(need, z, (0, 1) if LINE_COLUMNS > 1 else (0, 1, 2)))
+            if LINE_COLUMNS > 1:
+                second = rows_dev * LINE_COLUMNS // 2
+                pl.when(e == second)(functools.partial(need, z, (2,)))
 
             @pl.when((u == 0) & (h == 0))
             def _():
@@ -646,7 +650,7 @@
 
             terms[...] = jnp.dot(
                 attn[rows, :],
-                wo[:, pl.ds(pl.multiple_of(z * chunk + h * wide_half, 128), wide_half)],
+                wo[:, pl.ds(pl.multiple_of(z * chunk + h * line_width, 128), line_width)],
                 preferred_element_type=jnp.float32,
             )
             for side in range(2):
@@ -801,8 +805,8 @@
         attn_shape = (tok_dev, 2 * q_width)
         wo_shape = (2 * out_rows, width // 2)
         sums_shape = (2, line, tok_dev, width_local)
-        terms_shape = (ROW_TOKENS, width_local // 2)
-        sum_sems = (2, line, 2 * (tok_dev // ROW_TOKENS))
+        terms_shape = (ROW_TOKENS, width_local // LINE_COLUMNS)
+        sum_sems = (2, line, LINE_COLUMNS * (tok_dev // ROW_TOKENS))
     else:
         kinds = 3 * PARTS + COLUMNS
         attn_shape = (tok_dev, q_width)

time: 190 us -> 188 us (0.989)
  Pallas kernels: 188 us -> 186 us
where the time goes in v4:
time: 188 us; the launch traced here: 187 us
  Pallas kernels  186 us (99%)
    pallas_call x1, Pallas kernels, local(): pl.pallas_call(functools.partial(kernel, dp_count, mp_count), out_shape=p...  186 us

profile of v4, /device:TPU:15, one launch (start us, length us, event | category | flops | bytes accessed | tf_op | source)
XLA Modules:
  0.0 187.0 jit_solution(17807995556131650375)
XLA Ops:
  0.0 186.0 %shard_map.100 = bf16[512,1024]{1,0:T(8,128)(2,1)S(1)} custom-call(s32[64]{0:T(128)} %row_ref.1, s32[2,64]{1,0:T(2,128)} %bitcast.5, bf16[16,48,1024]{2,1,0:T(8,128)(2,1)} %tok_ref.1, f32[1,8192]{1,0:T(1,128)} %bitcast.3, bf16[2048,512]{1,0:T(8,128)(2,1)} %q_ref.1, bf16[2048,128]{1,0:T(8,128)(2,1)} %k_ref.1, bf16[2048,128]{1,0:T(8,128)(2,1)} %v_ref.1, ...), custom_call_target="tpu_custom_call" | custom-call | tf_op jit(solution)/shard_map/pallas_call | solution.py:822
  186.0 1.0 copy.12

commit v5 on v4

--- a/solution.py
+++ b/solution.py
@@ -12,7 +12,8 @@
 ROW_TOKENS = 128
 QUERY_PER_KV = 4
 SLICES = 2
-PARTS = 2
+PART_EDGES = (0, 2, 3, 4)
+PARTS = len(PART_EDGES) - 1
 COLUMNS = 4
 LINE_COLUMNS = 1
 UNITS = 2
@@ -76,7 +77,7 @@
     width = o_ref.shape[1]
     paired = pairs_up(n_dp, n_mp, width, chunk)
     slice_width = chunk // SLICES
-    part_rows = depth // PARTS
+    part_edges = [depth * e // PART_EDGES[-1] for e in PART_EDGES]
     unit = chunk // UNITS
     column = chunk // COLUMNS
     out_column = width // COLUMNS
@@ -94,7 +95,7 @@
     urgent = core == lead
     last = n_mp - 1
     final = 2 * last
-    part_slot = [min(2 * p, final - 1) for p in (4, n_mp)]
+    part_slot = [min(p, final - 1) for p in (8, 11, 2 * n_mp)]
 
     def token_slice(sub):
         return pl.ds(pl.multiple_of(sub * slice_width, 128), slice_width)
@@ -187,7 +188,8 @@
             start = owner * width + (kind - base) * out_column
             return wo.at[:, pl.ds(pl.multiple_of(start, 128), out_column)]
         p, which = divmod(kind, 3)
-        start = owner * depth + p * part_rows
+        start = owner * depth + part_edges[p]
+        part_rows = part_edges[p + 1] - part_edges[p]
         return wall.at[
             pl.ds(pl.multiple_of(start, 16), part_rows), pl.ds(starts[which], spans[which])
         ]
@@ -200,7 +202,9 @@
         if kind >= base:
             return o_ref.at[:, pl.ds((kind - base) * out_column, out_column)]
         p, which = divmod(kind, 3)
-        return (q_ref, k_ref, v_ref)[which].at[pl.ds(p * part_rows, part_rows), :]
+        return (q_ref, k_ref, v_ref)[which].at[
+            pl.ds(part_edges[p], part_edges[p + 1] - part_edges[p]), :
+        ]
 
     def weight_copy(kind, owner, source, target, slot, peer):
         return pltpu.make_async_remote_copy(
@@ -269,7 +273,7 @@
         for h in range(2):
             pl.when(inner | urgent)(mate_copy(h, at_x).start)
 
-    for kind in range(base // 2):
+    for kind in range(6):
         send_away(kind)
     for w in range(3):
         owns[w].start()
@@ -377,7 +381,7 @@
 
     lax.fori_loop(0, SLICES, ramp, 0)
 
-    for kind in range(base // 2, base):
+    for kind in range(6, base):
         send_away(kind)
     owns[3].start()
     for w in range(3):
@@ -429,7 +433,10 @@
             owner = start // depth
             near = (owner // 2 == group) & ((start + unit - 1) // depth // 2 == group)
             if depth % unit == 0:
-                needed = lax.rem(start + unit - 1, depth) // part_rows
+                needed = jnp.int32(0)
+                for p in range(1, PARTS):
+                    reached = lax.rem(start + unit - 1, depth) >= part_edges[p]
+                    needed = needed + jnp.where(reached, 1, 0)
             else:
                 needed = PARTS - 1
             when = part_slot[PARTS - 1]

time: 188 us -> 186 us (0.989)
  Pallas kernels: 186 us -> 184 us
where the time goes in v5:
time: 186 us; the launch traced here: 185 us
  Pallas kernels  184 us (99%)
    pallas_call x1, Pallas kernels, local(): pl.pallas_call(functools.partial(kernel, dp_count, mp_count), out_shape=p...  184 us

profile of v5, /device:TPU:15, one launch (start us, length us, event | category | flops | bytes accessed | tf_op | source)
XLA Modules:
  0.0 185.4 jit_solution(10876273212739085251)
XLA Ops:
  0.0 184.5 %shard_map.100 = bf16[512,1024]{1,0:T(8,128)(2,1)S(1)} custom-call(s32[64]{0:T(128)} %row_ref.1, s32[2,64]{1,0:T(2,128)} %bitcast.5, bf16[16,48,1024]{2,1,0:T(8,128)(2,1)} %tok_ref.1, f32[1,8192]{1,0:T(1,128)} %bitcast.3, bf16[2048,512]{1,0:T(8,128)(2,1)} %q_ref.1, bf16[2048,128]{1,0:T(8,128)(2,1)} %k_ref.1, bf16[2048,128]{1,0:T(8,128)(2,1)} %v_ref.1, ...), custom_call_target="tpu_custom_call" | custom-call | tf_op jit(solution)/shard_map/pallas_call | solution.py:829
  184.5 1.0 copy.12

commit v6 on v5

--- a/solution.py
+++ b/solution.py
@@ -521,7 +521,8 @@
             device_id_type=MESH,
         )
 
-    def attend(r, carry):
+    def mix(r):
+        found = []
         rows = pl.ds(pl.multiple_of(r * ROW_TOKENS, ROW_TOKENS), ROW_TOKENS)
         power = jnp.sum(square[rows, :], axis=1, keepdims=True)
         scale = lax.rsqrt(power / (n_mp * chunk) + 1e-05)
@@ -554,13 +555,20 @@
                 jnp.concatenate(probs, axis=0), value, preferred_element_type=jnp.float32
             ).astype(jnp.bfloat16)
             for i, h in enumerate(heads):
-                spot = pl.ds(pl.multiple_of(left + h * HEAD_SIZE, 128), HEAD_SIZE)
-                attn[rows, spot] = mixed[i * ROW_TOKENS:(i + 1) * ROW_TOKENS, :]
-        if paired:
-            share(r, at_x).start()
+                found.append((left + h * HEAD_SIZE, mixed[i * ROW_TOKENS:(i + 1) * ROW_TOKENS, :]))
+        return rows, found
+
+    def attend(t, carry):
+        both = [2 * t, 2 * t + 1]
+        results = [mix(r) for r in both]
+        for r, (rows, found) in zip(both, results):
+            for start, value in found:
+                attn[rows, pl.ds(pl.multiple_of(start, 128), HEAD_SIZE)] = value
+            if paired:
+                share(r, at_x).start()
         return carry
 
-    lax.fori_loop(0, tokens // ROW_TOKENS, attend, 0)
+    lax.fori_loop(0, rows_dev // 2, attend, 0)
     owns[3].wait()
 
     def line_copy(way, z, r):

time: 186 us -> 186 us (level)
  no operation moved by 1% of the time
where the time goes in v6:
time: 186 us
  Pallas kernels  185 us (99%)
    pallas_call x1, Pallas kernels, local(): pl.pallas_call(functools.partial(kernel, dp_count, mp_count), out_shape=p...  185 us

profile of v6, /device:TPU:15, one launch (start us, length us, event | category | flops | bytes accessed | tf_op | source)
XLA Modules:
  0.0 185.7 jit_solution(2524088936956564382)
XLA Ops:
  0.0 184.8 %shard_map.100 = bf16[512,1024]{1,0:T(8,128)(2,1)S(1)} custom-call(s32[64]{0:T(128)} %row_ref.1, s32[2,64]{1,0:T(2,128)} %bitcast.5, bf16[16,48,1024]{2,1,0:T(8,128)(2,1)} %tok_ref.1, f32[1,8192]{1,0:T(1,128)} %bitcast.3, bf16[2048,512]{1,0:T(8,128)(2,1)} %q_ref.1, bf16[2048,128]{1,0:T(8,128)(2,1)} %k_ref.1, bf16[2048,128]{1,0:T(8,128)(2,1)} %v_ref.1, ...), custom_call_target="tpu_custom_call" | custom-call | tf_op jit(solution)/shard_map/pallas_call | solution.py:837
  184.8 1.0 copy.12
